TPU v7x, 32 devices: a whole 2x2x4 slice. The times are simulated.
32 devices in a mesh: emit: 4 (over z), elem: 8 (over y, x, core).
Axes of the slice: x: 2, y: 2, z: 4, core: 2. Of those that a mesh axis runs over, the one named last changes fastest.
Arguments:
- traces: float32 [256, 1024, 1024], P('emit', 'elem'), may hold values from -6 to 6
- codes: float32 [4, 2, 128], replicated, may hold values from -0.5 to 0.5
- code_of: int32 [256], replicated, may hold values from 0 to 3
- order: int32 [256], replicated, may hold values from 0 to 255, each once
- steer: float32 [256, 1024, 256], P(None, 'elem'), may hold values from -0.1875 to 0.1875
Outputs:
- beams: float32 [256, 256, 256], P('elem', 'emit')
Inputs may be any that keep to these rules, and one draw needn't show every extreme that they name: `order`: each value 0 to 255 appears exactly once.
All inputs are finite; a program needn't handle non-finite values.
Results may differ from a plain program's by a relative error of at most 0.000071.
Values sent between devices are 32-bit elements; how exact they have to be, the bound alone decides.
No kernel may reach another device: no remote copies, remote signals or barrier semaphores. Data moves between devices by JAX's collectives and lax.ppermute only.
A program may use at most 320 MiB of HBM per device.

v0:
```python
import functools

import jax
import jax.numpy as jnp
import numpy as np
from jax import lax
from jax.experimental import pallas as pl
from jax.experimental.pallas import tpu as pltpu
from jax.sharding import PartitionSpec as P


ROWS = 8
VMEM_LIMIT = 24 * 1024 * 1024
ANY = pl.BlockSpec(memory_space=pl.ANY)


def split(value):
    high = value.astype(jnp.bfloat16)
    low = (value - high.astype(jnp.float32)).astype(jnp.bfloat16)
    return high, low


def dot(left, right):
    return lax.dot_general(left, right, (((1,), (0,)), ((), ())), preferred_element_type=jnp.float32)


def phase_table(samples, taps, freqs):
    freqs = np.concatenate([freqs, freqs])
    inner = np.arange(taps)[:, None] * freqs[None, :] % samples * (2 * np.pi / samples)
    outer = np.arange(samples // taps)[:, None] * taps * freqs[None, :] % samples * (2 * np.pi / samples)
    return np.concatenate([f(a).astype(np.float32) for a in (inner, outer) for f in (np.cos, np.sin)])


def folds(cls, nblock):
    half, quarter = nblock // 2, nblock // 4
    if cls % 2:
        return [([(1, half)], half)] + [([(1, j), (-1, j + half)], j) for j in range(1, half)]
    sign = 1 if cls == 0 else -1
    first = [(sign, quarter), (1, 2 * quarter), (sign, 3 * quarter)]
    return [(first, 0)] + [([(1, j)] + [(s, j + b) for s, b in first], j) for j in range(1, quarter)]


def spectral_kernel(base_ref, code_ref, x_ref, codes_hbm, table_hbm, *refs, scale, classes, tokens):
    count = len(classes)
    refs = refs[tokens:]
    outs, helds, (codes_ref, table_ref, sems) = refs[:count], refs[count : 2 * count], refs[2 * count :]
    rows, mdev, samples = x_ref.shape
    ncode, _, taps = codes_ref.shape
    nblock = samples // taps
    step = pl.program_id(0)

    @pl.when(step == 0)
    def _():
        copies = [pltpu.make_async_copy(codes_hbm, codes_ref, sems.at[0]), pltpu.make_async_copy(table_hbm, table_ref, sems.at[1])]
        for copy in copies:
            copy.start()
        for copy in copies:
            copy.wait()
        row = lax.broadcasted_iota(jnp.int32, (taps, taps), 0)
        col = lax.broadcasted_iota(jnp.int32, (taps, taps), 1)
        triangle = jnp.where(col <= row, 1.0, 0.0).astype(jnp.bfloat16)

        def build(code, carry):
            pair = codes_ref[code]
            ci, cq = (jnp.sum(jnp.where(row == col, pair[q : q + 1], 0.0), axis=1, keepdims=True) for q in (0, 1))
            for k, cls in enumerate(classes):
                cosine, sine = table_ref[k, :taps], table_ref[k, taps : 2 * taps]
                wcos_ref, wsin_ref = (table_ref.at[k, pl.ds(2 * taps + q * nblock, nblock)] for q in (0, 1))
                width = cosine.shape[1]
                left = lax.broadcasted_iota(jnp.int32, (taps, width), 1) < width // 2
                terms = split(jnp.concatenate([ci * cosine - cq * sine, ci * sine + cq * cosine], axis=1))
                summed = (dot(triangle, terms[0]) + dot(triangle, terms[1])) * scale
                pr, pi = summed[:, :width], summed[:, width:]
                sums = folds(cls, nblock)
                depth = (1 + len(sums)) * taps

                def put(place, value):
                    high, low = split(value)
                    both = jnp.concatenate([high, low], axis=1)
                    helds[k][code, pl.ds(place * taps, taps), :] = both
                    helds[k][code, pl.ds(depth + place * taps, taps), :] = both

                put(0, jnp.where(left, cosine * pr + sine * pi, cosine * pi - sine * pr))
                gr, gi = pr[taps - 1 :, :], pi[taps - 1 :, :]
                br, bi = cosine * gr + sine * gi, cosine * gi - sine * gr
                for place, (_, power) in enumerate(sums):
                    wr, wi = wcos_ref[power : power + 1, :], wsin_ref[power : power + 1, :]
                    put(1 + place, jnp.where(left, br * wr + bi * wi, bi * wr - br * wi))
            return carry

        lax.fori_loop(0, ncode, build, 0)

    for e in range(rows):
        code = code_ref[base_ref[0] + step * rows + e]
        for k, cls in enumerate(classes):
            parts = [x_ref[e, :, :taps]]
            for terms, _ in folds(cls, nblock):
                total = None
                for sign, b in terms:
                    block = x_ref[e, :, b * taps : (b + 1) * taps]
                    if total is None:
                        total = block if sign > 0 else -block
                    else:
                        total = total + block if sign > 0 else total - block
                parts.append(total)
            pairs = [split(p) for p in parts]
            source = jnp.concatenate([h for h, _ in pairs] + [l for _, l in pairs], axis=1)
            both = dot(source, helds[k][code])
            width = both.shape[1] // 2
            flat = outs[k].reshape(width * rows, mdev)
            flat[pl.ds(e, width, stride=rows), :] = (both[:, :width] + both[:, width:]).T


def spectra_of(traces, codes, code_of, base, classes, bins, scale, after):
    edev, mdev, samples = traces.shape
    ncode, _, taps = codes.shape
    rows = ROWS
    table = jnp.asarray(np.stack([phase_table(samples, taps, np.arange(cls, bins, 4) - bins // 2) for cls in classes]))
    width = 2 * (bins // 4)

    hbm = pl.BlockSpec(memory_space=pltpu.HBM)
    depths = [2 * (1 + len(folds(cls, samples // taps))) * taps for cls in classes]
    return pl.pallas_call(
        functools.partial(spectral_kernel, scale=scale, classes=classes, tokens=len(after)),
        grid_spec=pltpu.PrefetchScalarGridSpec(
            num_scalar_prefetch=2,
            grid=(edev // rows,),
            in_specs=[pl.BlockSpec((rows, mdev, samples), lambda i, *s: (i, 0, 0)), hbm, hbm] + [ANY] * len(after),
            out_specs=[pl.BlockSpec((width, rows, mdev), lambda i, *s: (0, i, 0))] * len(classes),
            scratch_shapes=[pltpu.VMEM((ncode, depth, 2 * width), jnp.bfloat16) for depth in depths]
            + [pltpu.VMEM(codes.shape, jnp.float32), pltpu.VMEM(table.shape, jnp.float32), pltpu.SemaphoreType.DMA((2,))],
        ),
        out_shape=[jax.ShapeDtypeStruct((width, edev, mdev), jnp.float32)] * len(classes),
        compiler_params=pltpu.CompilerParams(vmem_limit_bytes=VMEM_LIMIT),
        cost_estimate=pl.CostEstimate(
            flops=edev * mdev * sum(depths) * 2 * width * 2,
            bytes_accessed=traces.size * 4 + len(classes) * width * edev * mdev * 4, transcendentals=0,
        ),
        name="spectral",
    )(base, code_of, traces, codes, table, *after)


def steer_kernel(target_ref, *refs, tokens):
    spectra_refs, steer_refs = refs[:2], refs[2:4]
    sent_ref, kept_ref = refs[4 + tokens :]
    nb, _, width = steer_refs[0].shape
    half = width // 2
    step, steps = pl.program_id(0), pl.num_programs(0)

    def complex_rows(w):
        return jnp.concatenate([w, jnp.concatenate([-w[:, half:], w[:, :half]], axis=1)], axis=0)

    def compute(out_ref):
        for k in range(2):
            for i in range(nb):
                wh, wl = split(steer_refs[k][i])
                sh, sl = split(jnp.concatenate([spectra_refs[k][0, i], spectra_refs[k][1, i]], axis=1))
                edev = sh.shape[0]
                both = dot(jnp.concatenate([sh, sl], axis=0), complex_rows(wh))
                out_ref[k, i] = both[:edev] + both[edev:] + dot(sh, complex_rows(wl))

    @pl.when(step < steps // 2)
    def _():
        compute(sent_ref)

    @pl.when(step >= steps // 2)
    def _():
        compute(kept_ref)


def steer_blocks(targets, spectra, steer, cls, after):
    count = targets.shape[0] // 2
    _, total, edev, mdev = spectra.shape
    nb = total // (2 * count)
    width = steer.shape[3]
    edge = count // 2
    shape = jax.ShapeDtypeStruct((count, nb, edev, width), jnp.float32)
    return pl.pallas_call(
        functools.partial(steer_kernel, tokens=len(after)),
        grid_spec=pltpu.PrefetchScalarGridSpec(
            num_scalar_prefetch=1,
            grid=(count,),
            in_specs=[pl.BlockSpec((2, nb, edev, mdev), lambda i, t, k=k: (0, t[2 * i + k], 0, 0)) for k in range(2)]
            + [pl.BlockSpec((nb, None, mdev, width), lambda i, t, k=k: (t[2 * i + k], cls, 0, 0)) for k in range(2)]
            + [ANY] * len(after),
            out_specs=[
                pl.BlockSpec((2, nb, edev, width), lambda i, t: (jnp.minimum(i, edge - 1), 0, 0, 0)),
                pl.BlockSpec((2, nb, edev, width), lambda i, t: (jnp.maximum(i - edge, 0), 0, 0, 0)),
            ],
        ),
        out_shape=[shape, shape],
        compiler_params=pltpu.CompilerParams(vmem_limit_bytes=VMEM_LIMIT),
        cost_estimate=pl.CostEstimate(
            flops=total * edev * 2 * mdev * width * 2 * 3,
            bytes_accessed=4 * total * (2 * edev * mdev + mdev * width + edev * width), transcendentals=0,
        ),
        name="steer",
    )(targets, spectra, spectra, steer, steer, *after)


def decode_kernel(signs_ref, own_ref, near_ref, *refs, tokens):
    outs = refs[tokens:]
    nb = own_ref.shape[0]
    count, kdev, _ = signs_ref.shape
    signs = signs_ref[...].reshape(count * kdev, signs_ref.shape[2])
    for i in range(nb):
        high, low = split(jnp.concatenate([own_ref[i], near_ref[i]], axis=0))
        result = dot(signs, high) + dot(signs, low)
        for j in range(count):
            outs[j][i] = result[j * kdev : (j + 1) * kdev]


def decode(signs, own, near, after):
    nb, _, width = own.shape
    count, kdev, _ = signs.shape
    vmem = pl.BlockSpec(memory_space=pltpu.VMEM)
    return pl.pallas_call(
        functools.partial(decode_kernel, tokens=len(after)),
        in_specs=[vmem] * 3 + [ANY] * len(after),
        out_shape=[jax.ShapeDtypeStruct((nb, kdev, width), jnp.float32)] * count,
        compiler_params=pltpu.CompilerParams(vmem_limit_bytes=VMEM_LIMIT),
        cost_estimate=pl.CostEstimate(
            flops=signs.size * nb * width * 4, bytes_accessed=4 * (2 * own.size + count * nb * kdev * width), transcendentals=0
        ),
        name="decode",
    )(signs, own, near, *after)


def finish_kernel(*refs, scale, held):
    parts, out_ref = refs[held:-1], refs[-1]
    total = parts[0][...]
    for part in parts[1:]:
        total = total + part[...]
    out_ref[...] = total * scale


def finish(beams, own, arrived, cls, scale):
    nb, kdev, width = own.shape
    block = pl.BlockSpec((nb, kdev, width), lambda i: (0, 0, 0))
    held = [] if beams is None else [beams]
    return pl.pallas_call(
        functools.partial(finish_kernel, scale=scale, held=len(held)),
        grid=(1,),
        in_specs=[ANY] * len(held) + [block] * (1 + len(arrived)),
        out_specs=pl.BlockSpec((nb, None, kdev, width), lambda i: (0, cls, 0, 0)),
        out_shape=jax.ShapeDtypeStruct((nb, 4, kdev, width), jnp.float32),
        input_output_aliases={0: 0} if held else {},
        compiler_params=pltpu.CompilerParams(vmem_limit_bytes=VMEM_LIMIT),
        cost_estimate=pl.CostEstimate(
            flops=2 * nb * kdev * width, bytes_accessed=4 * (2 + len(arrived)) * nb * kdev * width, transcendentals=0
        ),
        name="finish",
    )(*held, own, *arrived)


def per_device(traces, codes, code_of, order, steer):
    edev, mdev, samples = traces.shape
    emissions = order.shape[0]
    bins = steer.shape[0]
    ne, nm = lax.axis_size("emit"), lax.axis_size("elem")
    me = lax.axis_index("elem")
    here = lax.axis_index("emit")
    base = (here * edev).reshape(1).astype(jnp.int32)
    steer = steer.reshape(bins // 4, 4, *steer.shape[1:])

    nbit = nm.bit_length() - 1
    upper = list(range(1, nbit))
    orders = (upper, upper[::-1])
    nrel = 1 << (nbit - 1)

    def mask_of(core, rel):
        return sum((rel >> (nbit - 2 - s) & 1) << bit for s, bit in enumerate(orders[core]))

    masks = np.array([[mask_of(core, nrel - 1 - p) for p in range(nrel)] for core in (0, 1)], np.int32)
    masks = np.stack([np.concatenate([1 ^ masks[1 - core], masks[core]]) for core in (0, 1)])
    targets = me ^ jnp.where(me & 1 == 0, masks[0], masks[1])
    swaps = [[(i, i ^ 1) for i in range(nm)]]
    for s in range(nbit - 1):
        swaps.append([(i, i ^ (1 << orders[i & 1][s])) for i in range(nm)])

    def signs_of(gap):
        rows = jnp.concatenate([lax.dynamic_slice_in_dim(order, z * edev, edev) for z in (here, here ^ gap)])
        others = others_of(gap, ne)
        wanted = jnp.stack([here ^ z for z in others + [0]])
        columns = wanted[:, None] * edev + jnp.arange(edev, dtype=jnp.int32)[None, :]
        parity = lax.population_count(columns[:, :, None] & rows[None, None, :]) & 1
        return others, (1 - 2 * parity).astype(jnp.bfloat16)

    scale = float(np.float32(1.0) / np.sqrt(np.float32(samples)))
    shrink = float(1.0 / np.sqrt(np.float32(emissions)))
    gaps = {cls: gap_of(cls, ne) for cls in range(4)}
    signs = {gap: signs_of(gap) for gap in sorted(set(gaps.values()))}

    last = []
    state = {cls: {} for cls in range(4)}
    beams = None

    def spectral(*classes):
        nonlocal last
        out = spectra_of(traces, codes, code_of, base, classes, bins, scale, last)
        for cls, spectra in zip(classes, out):
            state[cls]["spectra"] = spectra.reshape(2, bins // 4, edev, mdev)
        last = [out[0]]

    def steered(cls):
        nonlocal last
        sent, kept = steer_blocks(targets, state[cls]["spectra"], steer, cls, last)
        last = [sent]
        state[cls]["kept"] = kept
        state[cls]["arrived"] = [lax.ppermute(sent, "elem", swaps[0])]

    def added(cls):
        nonlocal last
        kept, arrived = state[cls]["kept"], state[cls]["arrived"]
        stage = len(arrived)
        high = nrel >> (stage - 1)
        low = high >> 1
        kept, _ = lax.optimization_barrier((kept, last[0]))
        total = kept[nrel - high : nrel - low]
        for k, array in enumerate(arrived):
            start = (nrel >> k) - high
            total = total + array[start : start + high - low]
        last = [total]
        if stage < nbit:
            arrived.append(lax.ppermute(total, "elem", swaps[stage]))
        else:
            own = total[0]
            state[cls]["own"] = own
            state[cls]["near"] = lax.ppermute(own, "emit", [(z, z ^ gaps[cls]) for z in range(ne)])

    def decoded(cls):
        nonlocal last
        others, held = signs[gaps[cls]]
        out = decode(held, state[cls]["own"], state[cls]["near"], last)
        last = [out[0]]
        state[cls]["partial"] = out[-1]
        state[cls]["fetched"] = [
            lax.ppermute(part, "emit", [(z, z ^ gap) for z in range(ne)]) for part, gap in zip(out, others)
        ]

    def finished(cls):
        nonlocal beams
        beams = finish(beams, state[cls]["partial"], state[cls]["fetched"], cls, shrink)

    steps = {"spectral": spectral, "steer": steered, "sum": added, "decode": decoded, "finish": finished}
    for name, *values in plan(nbit):
        steps[name](*values)
    return beams.reshape(-1, *beams.shape[2:])


def plan(nbit):
    more = range(nbit - 2)
    return [
        ("spectral", 2, 0), ("steer", 2), ("steer", 0), ("sum", 2),
        ("spectral", 1), *(("sum", 2) for _ in more), ("sum", 0), ("steer", 1), ("sum", 2),
        ("spectral", 3), *(("sum", 0) for _ in more), ("sum", 1), ("steer", 3), ("sum", 0),
        ("decode", 2), ("sum", 3), *(("sum", 1) for _ in more), ("sum", 1), *(("sum", 3) for _ in more),
        ("decode", 0), ("decode", 1), ("sum", 3), ("decode", 3),
        ("finish", 2), ("finish", 0), ("finish", 1), ("finish", 3),
    ]


def gap_of(cls, ne):
    return ne // 2 if cls in (2, 0) else 1


def others_of(gap, ne):
    return [z for z in range(1, ne) if not z & gap]


def solution(mesh):
    placed = (P("emit", "elem", None), P(), P(), P(), P(None, "elem", None))

    return jax.shard_map(per_device, mesh=mesh, in_specs=placed, out_specs=P("elem", "emit", None), check_vma=False)
```

profile of v0, /device:TPU:0, one launch (start us, length us, event | category | flops | bytes accessed | tf_op | source)
XLA Modules:
  0.0 235.6 jit_solution(1112530420829648793)
XLA Ops:
  0.7 1.0 copy-done.5
  3.0 18.3 %spectral.3 = (f32[128,64,128]{2,1,0:T(8,128)S(1)}, f32[128,64,128]{2,1,0:T(8,128)S(1)}) custom-call(s32[1]{0:T(128)} %bitcast.2.base_ref, s32[256]{0:T(256)S(1)} %copy-done.10, f32[64,128,1024]{2,1,0:T(8,128)} %x_ref.5, f32[4,2,128]{2,1,0:T(2,128)S(1)} %copy-done.8, f32[2,272,128]{2,1,0:T(8,128)S(1)} %copy-done.5), custom_call_target="tpu_custom_call" | custom-call | flops 6442450944 | bytes 41943040 | tf_op jit(solution)/shard_map/spectral/pallas_call | solution.py:123
  21.3 6.6 %steer.4 = (f32[4,8,64,256]{3,2,1,0:T(8,128)S(1)}, f32[4,8,64,256]{3,2,1,0:T(8,128)S(1)}) custom-call(s32[8]{0:T(128)S(1)} %fusion.4.target_ref, f32[2,64,64,128]{3,2,1,0:T(8,128)S(1)} %bitcast.14, f32[2,64,64,128]{3,2,1,0:T(8,128)S(1)} %bitcast.15, f32[64,4,128,256]{3,2,1,0:T(8,128)} %bitcast.30, f32[64,4,128,256]{3,2,1,0:T(8,128)} %bitcast.31, ...), custom_call_target="tpu_custom_call" | custom-call | flops 1610612736 | bytes 16777216 | tf_op jit(solution)/shard_map/steer/pallas_call | solution.py:178
  28.4 6.6 %steer.5 = (f32[4,8,64,256]{3,2,1,0:T(8,128)S(1)}, f32[4,8,64,256]{3,2,1,0:T(8,128)S(1)}) custom-call(s32[8]{0:T(128)S(1)} %fusion.4.target_ref, f32[2,64,64,128]{3,2,1,0:T(8,128)S(1)} %bitcast.20, f32[2,64,64,128]{3,2,1,0:T(8,128)S(1)} %bitcast.21, f32[64,4,128,256]{3,2,1,0:T(8,128)} %bitcast.32, f32[64,4,128,256]{3,2,1,0:T(8,128)} %bitcast.33, ...), custom_call_target="tpu_custom_call" | custom-call | flops 1610612736 | bytes 16777216 | tf_op jit(solution)/shard_map/steer/pallas_call | solution.py:178
  35.3 3.0 %collective-permute-start.1 = (f32[2,8,64,256]{3,2,1,0:T(8,128)S(1)}, f32[2,8,64,256]{3,2,1,0:T(8,128)S(1)}, u32[]{:S(2)}, u32[]{:S(2)}) collective-permute-start(f32[2,8,64,256]{3,2,1,0:T(8,128)S(1)} %slice_add_fusion.3.refs_0_), channel_id=1, source_target_pairs={{0,2},{1,5},{2,0},{3,7},{4,6},{5,1},{6,4},{7,3},{8,10},{9,13},{10,... | collective-permute-start | bytes 3145736 | tf_op jit(solution)/shard_map/ppermute | solution.py:325
  38.4 17.1 %spectral.4 = f32[128,64,128]{2,1,0:T(8,128)S(1)} custom-call(s32[1]{0:T(128)} %bitcast.2.base_ref, s32[256]{0:T(256)S(1)} %copy-done.11, f32[64,128,1024]{2,1,0:T(8,128)} %x_ref.5, f32[4,2,128]{2,1,0:T(2,128)S(1)} %copy-done.9, f32[1,272,128]{2,1,0:T(8,128)S(1)} %copy-done.7, f32[2,8,64,256]{3,2,1,0:T(8,128)S(1)} %slice_add_fusion.3.refs_0_), custom_call_target="tpu_custom_call" | custom-call | flops 5368709120 | bytes 37748736 | tf_op jit(solution)/shard_map/spectral/pallas_call | solution.py:123
  55.8 6.6 %steer.6 = (f32[4,8,64,256]{3,2,1,0:T(8,128)S(1)}, f32[4,8,64,256]{3,2,1,0:T(8,128)S(1)}) custom-call(s32[8]{0:T(128)S(1)} %fusion.4.target_ref, f32[2,64,64,128]{3,2,1,0:T(8,128)S(1)} %bitcast.18, f32[2,64,64,128]{3,2,1,0:T(8,128)S(1)} %bitcast.19, f32[64,4,128,256]{3,2,1,0:T(8,128)} %bitcast.34, f32[64,4,128,256]{3,2,1,0:T(8,128)} %bitcast.35, ...), custom_call_target="tpu_custom_call" | custom-call | flops 1610612736 | bytes 16777216 | tf_op jit(solution)/shard_map/steer/pallas_call | solution.py:178
  62.6 1.6 collective-permute-start.3
  64.8 12.6 %collective-permute-done.3 = f32[1,8,64,256]{3,2,1,0:T(8,128)S(1)} collective-permute-done((f32[1,8,64,256]{3,2,1,0:T(8,128)S(1)}, f32[1,8,64,256]{3,2,1,0:T(8,128)S(1)}, u32[]{:S(2)}, u32[]{:S(2)}) %collective-permute-start.3) | collective-permute-done | bytes 524320 | tf_op jit(solution)/shard_map/ppermute | solution.py:325
  77.6 17.1 %spectral.5 = f32[128,64,128]{2,1,0:T(8,128)S(1)} custom-call(s32[1]{0:T(128)} %bitcast.2.base_ref, s32[256]{0:T(256)S(1)} %copy-done.11, f32[64,128,1024]{2,1,0:T(8,128)} %x_ref.5, f32[4,2,128]{2,1,0:T(2,128)S(1)} %copy-done.9, f32[1,272,128]{2,1,0:T(8,128)S(1)} %copy-done.6, f32[1,8,64,256]{3,2,1,0:T(8,128)S(1)} %fusion.3.refs_0_), custom_call_target="tpu_custom_call" | custom-call | flops 5368709120 | bytes 37748736 | tf_op jit(solution)/shard_map/spectral/pallas_call | solution.py:123
  95.8 7.6 %steer.7 = (f32[4,8,64,256]{3,2,1,0:T(8,128)}, f32[4,8,64,256]{3,2,1,0:T(8,128)S(1)}) custom-call(s32[8]{0:T(128)S(1)} %fusion.4.target_ref, f32[2,64,64,128]{3,2,1,0:T(8,128)S(1)} %bitcast.16, f32[2,64,64,128]{3,2,1,0:T(8,128)S(1)} %bitcast.17, f32[64,4,128,256]{3,2,1,0:T(8,128)} %bitcast.36, f32[64,4,128,256]{3,2,1,0:T(8,128)} %bitcast.37, ...), custom_call_target="tpu_custom_call" | custom-call | flops 1610612736 | bytes 16777216 | tf_op jit(solution)/shard_map/steer/pallas_call | solution.py:178
  103.5 1.4 copy-done
  104.9 1.6 collective-permute-start.7
  106.7 2.6 %collective-permute-start.4 = (f32[8,64,256]{2,1,0:T(8,128)S(1)}, f32[8,64,256]{2,1,0:T(8,128)S(1)}, u32[]{:S(2)}, u32[]{:S(2)}) collective-permute-start(f32[8,64,256]{2,1,0:T(8,128)S(1)} %bitcast.22), channel_id=1, source_target_pairs={{0,16},{8,24},{16,0},{24,8},{1,17},{9,25},{17,1},{25,9},{2,18},{10... | collective-permute-start | bytes 1572872 | tf_op jit(solution)/shard_map/ppermute | solution.py:329
  109.5 10.1 %collective-permute-done.7 = f32[1,8,64,256]{3,2,1,0:T(8,128)S(1)} collective-permute-done((f32[1,8,64,256]{3,2,1,0:T(8,128)}, f32[1,8,64,256]{3,2,1,0:T(8,128)S(1)}, u32[]{:S(2)}, u32[]{:S(2)}) %collective-permute-start.7) | collective-permute-done | bytes 524320 | tf_op jit(solution)/shard_map/ppermute | solution.py:325
  119.6 1.3 fusion.2.refs_0_
  121.0 11.9 %collective-permute-done.4.near_ref = f32[8,64,256]{2,1,0:T(8,128)S(1)} collective-permute-done((f32[8,64,256]{2,1,0:T(8,128)S(1)}, f32[8,64,256]{2,1,0:T(8,128)S(1)}, u32[]{:S(2)}, u32[]{:S(2)}) %collective-permute-start.4) | collective-permute-done | bytes 524320 | tf_op jit(solution)/shard_map/ppermute | solution.py:329
  133.3 1.4 slice_add_fusion
  134.7 1.8 collective-permute-start.13
  137.2 14.3 %collective-permute-done.12 = f32[1,8,64,256]{3,2,1,0:T(8,128)S(1)} collective-permute-done((f32[1,8,64,256]{3,2,1,0:T(8,128)S(1)}, f32[1,8,64,256]{3,2,1,0:T(8,128)S(1)}, u32[]{:S(2)}, u32[]{:S(2)}) %collective-permute-start.12) | collective-permute-done | bytes 524320 | tf_op jit(solution)/shard_map/ppermute | solution.py:325
  152.3 2.2 collective-permute-done.13
  154.6 1.1 slice_add_fusion.6.refs_0_
  155.7 0.9 collective-permute-start.17
  156.8 4.9 %collective-permute-done.9.near_ref = f32[8,64,256]{2,1,0:T(8,128)S(1)} collective-permute-done((f32[8,64,256]{2,1,0:T(8,128)S(1)}, f32[8,64,256]{2,1,0:T(8,128)S(1)}, u32[]{:S(2)}, u32[]{:S(2)}) %collective-permute-start.9) | collective-permute-done | bytes 524320 | tf_op jit(solution)/shard_map/ppermute | solution.py:329
  162.2 10.1 %collective-permute-done.15.near_ref = f32[8,64,256]{2,1,0:T(8,128)S(1)} collective-permute-done((f32[8,64,256]{2,1,0:T(8,128)S(1)}, f32[8,64,256]{2,1,0:T(8,128)S(1)}, u32[]{:S(2)}, u32[]{:S(2)}) %collective-permute-start.15) | collective-permute-done | bytes 524320 | tf_op jit(solution)/shard_map/ppermute | solution.py:329
  172.7 1.2 fusion.refs_0_
  174.0 2.0 collective-permute-start.8
  176.1 2.3 collective-permute-start.16
  178.4 21.7 %collective-permute-done.18.near_ref = f32[8,64,256]{2,1,0:T(8,128)S(1)} collective-permute-done((f32[8,64,256]{2,1,0:T(8,128)S(1)}, f32[8,64,256]{2,1,0:T(8,128)S(1)}, u32[]{:S(2)}, u32[]{:S(2)}) %collective-permute-start.18) | collective-permute-done | bytes 524320 | tf_op jit(solution)/shard_map/ppermute | solution.py:329
  200.5 20.1 %collective-permute-done.8.refs_1_ = f32[8,64,256]{2,1,0:T(8,128)S(1)} collective-permute-done((f32[8,64,256]{2,1,0:T(8,128)S(1)}, f32[8,64,256]{2,1,0:T(8,128)S(1)}, u32[]{:S(2)}, u32[]{:S(2)}) %collective-permute-start.8) | collective-permute-done | bytes 524320 | tf_op jit(solution)/shard_map/ppermute | solution.py:338
  221.5 8.8 %collective-permute-done.14.refs_2_ = f32[8,64,256]{2,1,0:T(8,128)S(1)} collective-permute-done((f32[8,64,256]{2,1,0:T(8,128)S(1)}, f32[8,64,256]{2,1,0:T(8,128)S(1)}, u32[]{:S(2)}, u32[]{:S(2)}) %collective-permute-start.14) | collective-permute-done | bytes 524320 | tf_op jit(solution)/shard_map/ppermute | solution.py:338
  232.0 2.8 %collective-permute-done.19.refs_2_ = f32[8,64,256]{2,1,0:T(8,128)S(1)} collective-permute-done((f32[8,64,256]{2,1,0:T(8,128)S(1)}, f32[8,64,256]{2,1,0:T(8,128)S(1)}, u32[]{:S(2)}, u32[]{:S(2)}) %collective-permute-start.19) | collective-permute-done | bytes 524320 | tf_op jit(solution)/shard_map/ppermute | solution.py:338
  (75 shorter events, 12.6 us)
Async XLA Ops:
  27.9 7.3 %collective-permute-start = (f32[4,8,64,256]{3,2,1,0:T(8,128)S(1)}, f32[4,8,64,256]{3,2,1,0:T(8,128)S(1)}, u32[]{:S(2)}, u32[]{:S(2)}) collective-permute-start(f32[4,8,64,256]{3,2,1,0:T(8,128)S(1)} %get-tuple-element.38.refs_4_), channel_id=1, source_target_pairs={{0,1},{1,0},{2,3},{3,2},{4,5},{5,4},{6,7},{7,6},{8,9},{9,8},{10,11... | collective-permute-start | bytes 6291464 | tf_op jit(solution)/shard_map/ppermute | solution.py:310
  35.0 59.7 %copy-start.4 = (f32[4,8,64,256]{3,2,1,0:T(8,128)}, f32[4,8,64,256]{3,2,1,0:T(8,128)S(1)}, u32[]{:S(2)}) copy-start(f32[4,8,64,256]{3,2,1,0:T(8,128)S(1)} %get-tuple-element.50) | copy-start | bytes 6291460
  35.1 3.3 %copy-start.7 = (f32[1,272,128]{2,1,0:T(8,128)S(1)}, f32[1,272,128]{2,1,0:T(8,128)}, u32[]{:S(2)}) copy-start(f32[1,272,128]{2,1,0:T(8,128)} %constant.34.clone.table_hbm) | copy-start | bytes 417796
  35.1 3.3 %copy-start.9 = (f32[4,2,128]{2,1,0:T(2,128)S(1)}, f32[4,2,128]{2,1,0:T(2,128)}, u32[]{:S(2)}) copy-start(f32[4,2,128]{2,1,0:T(2,128)} %codes_hbm.5) | copy-start | bytes 12292
  35.1 3.3 %copy-start.11 = (s32[256]{0:T(256)S(1)}, s32[256]{0:T(256)}, u32[]{:S(2)}) copy-start(s32[256]{0:T(256)} %code_ref.5) | copy-start | bytes 3076
  35.1 20.6 %collective-permute-start.2 = (f32[4,8,64,256]{3,2,1,0:T(8,128)S(1)}, f32[4,8,64,256]{3,2,1,0:T(8,128)S(1)}, u32[]{:S(2)}, u32[]{:S(2)}) collective-permute-start(f32[4,8,64,256]{3,2,1,0:T(8,128)S(1)} %get-tuple-element.39), channel_id=1, source_target_pairs={{0,1},{1,0},{2,3},{3,2},{4,5},{5,4},{6,7},{7,6},{8,9},{9,8},{10,11... | collective-permute-start | bytes 6291464 | tf_op jit(solution)/shard_map/ppermute | solution.py:310
  35.3 20.2 %collective-permute-start.1 = (f32[2,8,64,256]{3,2,1,0:T(8,128)S(1)}, f32[2,8,64,256]{3,2,1,0:T(8,128)S(1)}, u32[]{:S(2)}, u32[]{:S(2)}) collective-permute-start(f32[2,8,64,256]{3,2,1,0:T(8,128)S(1)} %slice_add_fusion.3.refs_0_), channel_id=1, source_target_pairs={{0,2},{1,5},{2,0},{3,7},{4,6},{5,1},{6,4},{7,3},{8,10},{9,13},{10,... | collective-permute-start | bytes 3145736 | tf_op jit(solution)/shard_map/ppermute | solution.py:325
  55.7 39.1 %copy-start.14 = (f32[4,8,64,256]{3,2,1,0:T(8,128)}, f32[4,8,64,256]{3,2,1,0:T(8,128)S(1)}, u32[]{:S(2)}) copy-start(f32[4,8,64,256]{3,2,1,0:T(8,128)S(1)} %collective-permute-done.2) | copy-start | bytes 6291460
  62.5 33.2 %copy-start.2 = (f32[4,8,64,256]{3,2,1,0:T(8,128)}, f32[4,8,64,256]{3,2,1,0:T(8,128)S(1)}, u32[]{:S(2)}) copy-start(f32[4,8,64,256]{3,2,1,0:T(8,128)S(1)} %get-tuple-element.56) | copy-start | bytes 6291460
  62.5 15.1 %copy-start.6 = (f32[1,272,128]{2,1,0:T(8,128)S(1)}, f32[1,272,128]{2,1,0:T(8,128)}, u32[]{:S(2)}) copy-start(f32[1,272,128]{2,1,0:T(8,128)} %constant.35.clone.table_hbm) | copy-start | bytes 417796
  62.5 33.2 %collective-permute-start.6 = (f32[4,8,64,256]{3,2,1,0:T(8,128)S(1)}, f32[4,8,64,256]{3,2,1,0:T(8,128)S(1)}, u32[]{:S(2)}, u32[]{:S(2)}) collective-permute-start(f32[4,8,64,256]{3,2,1,0:T(8,128)S(1)} %get-tuple-element.44), channel_id=1, source_target_pairs={{0,1},{1,0},{2,3},{3,2},{4,5},{5,4},{6,7},{7,6},{8,9},{9,8},{10,11... | collective-permute-start | bytes 6291464 | tf_op jit(solution)/shard_map/ppermute | solution.py:310
  62.6 14.8 %collective-permute-start.3 = (f32[1,8,64,256]{3,2,1,0:T(8,128)S(1)}, f32[1,8,64,256]{3,2,1,0:T(8,128)S(1)}, u32[]{:S(2)}, u32[]{:S(2)}) collective-permute-start(f32[1,8,64,256]{3,2,1,0:T(8,128)S(1)} %slice_add_fusion.18), channel_id=1, source_target_pairs={{0,4},{1,3},{2,6},{3,1},{4,0},{5,7},{6,2},{7,5},{8,12},{9,11},{10,... | collective-permute-start | bytes 1572872 | tf_op jit(solution)/shard_map/ppermute | solution.py:325
  64.2 30.6 %collective-permute-start.5 = (f32[2,8,64,256]{3,2,1,0:T(8,128)S(1)}, f32[2,8,64,256]{3,2,1,0:T(8,128)S(1)}, u32[]{:S(2)}, u32[]{:S(2)}) collective-permute-start(f32[2,8,64,256]{3,2,1,0:T(8,128)S(1)} %slice_add_fusion.2.refs_4_), channel_id=1, source_target_pairs={{0,2},{1,5},{2,0},{3,7},{4,6},{5,1},{6,4},{7,3},{8,10},{9,13},{10,... | collective-permute-start | bytes 3145736 | tf_op jit(solution)/shard_map/ppermute | solution.py:325
  95.7 7.8 %copy-start.12 = (f32[4,8,64,256]{3,2,1,0:T(8,128)}, f32[4,8,64,256]{3,2,1,0:T(8,128)S(1)}, u32[]{:S(2)}) copy-start(f32[4,8,64,256]{3,2,1,0:T(8,128)S(1)} %collective-permute-done.6) | copy-start | bytes 6291460
  95.8 10.8 %copy-start.15 = (s32[256]{0:T(256)S(1)}, s32[256]{0:T(256)}, u32[]{:S(2)}) copy-start(s32[256]{0:T(256)} %param.13) | copy-start | bytes 3076
  104.9 28.5 %collective-permute-start.10 = (f32[4,8,64,256]{3,2,1,0:T(8,128)}, f32[4,8,64,256]{3,2,1,0:T(8,128)}, u32[]{:S(2)}, u32[]{:S(2)}) collective-permute-start(f32[4,8,64,256]{3,2,1,0:T(8,128)} %get-tuple-element.49), channel_id=1, source_target_pairs={{0,1},{1,0},{2,3},{3,2},{4,5},{5,4},{6,7},{7,6},{8,9},{9,8},{10,11... | collective-permute-start | bytes 6291464 | tf_op jit(solution)/shard_map/ppermute | solution.py:310
  104.9 14.7 %collective-permute-start.7 = (f32[1,8,64,256]{3,2,1,0:T(8,128)}, f32[1,8,64,256]{3,2,1,0:T(8,128)S(1)}, u32[]{:S(2)}, u32[]{:S(2)}) collective-permute-start(f32[1,8,64,256]{3,2,1,0:T(8,128)} %slice_add_fusion.14), channel_id=1, source_target_pairs={{0,4},{1,3},{2,6},{3,1},{4,0},{5,7},{6,2},{7,5},{8,12},{9,11},{10,... | collective-permute-start | bytes 1572872 | tf_op jit(solution)/shard_map/ppermute | solution.py:325
  106.6 29.9 %collective-permute-start.11 = (f32[2,8,64,256]{3,2,1,0:T(8,128)S(1)}, f32[2,8,64,256]{3,2,1,0:T(8,128)S(1)}, u32[]{:S(2)}, u32[]{:S(2)}) collective-permute-start(f32[2,8,64,256]{3,2,1,0:T(8,128)S(1)} %slice_add_fusion.1.refs_4_), channel_id=1, source_target_pairs={{0,2},{1,5},{2,0},{3,7},{4,6},{5,1},{6,4},{7,3},{8,10},{9,13},{10,... | collective-permute-start | bytes 3145736 | tf_op jit(solution)/shard_map/ppermute | solution.py:325
  106.7 26.1 %collective-permute-start.4 = (f32[8,64,256]{2,1,0:T(8,128)S(1)}, f32[8,64,256]{2,1,0:T(8,128)S(1)}, u32[]{:S(2)}, u32[]{:S(2)}) collective-permute-start(f32[8,64,256]{2,1,0:T(8,128)S(1)} %bitcast.22), channel_id=1, source_target_pairs={{0,16},{8,24},{16,0},{24,8},{1,17},{9,25},{17,1},{25,9},{2,18},{10... | collective-permute-start | bytes 1572872 | tf_op jit(solution)/shard_map/ppermute | solution.py:329
  109.5 23.8 %copy-start.1 = (f32[4,8,64,256]{3,2,1,0:T(8,128)S(1)}, f32[4,8,64,256]{3,2,1,0:T(8,128)}, u32[]{:S(2)}) copy-start(f32[4,8,64,256]{3,2,1,0:T(8,128)} %copy-done) | copy-start | bytes 6291460
  121.0 15.5 %copy-start.3 = (f32[4,8,64,256]{3,2,1,0:T(8,128)S(1)}, f32[4,8,64,256]{3,2,1,0:T(8,128)}, u32[]{:S(2)}) copy-start(f32[4,8,64,256]{3,2,1,0:T(8,128)} %copy-done.2) | copy-start | bytes 6291460
  121.0 15.5 %copy-start.13 = (f32[4,8,64,256]{3,2,1,0:T(8,128)S(1)}, f32[4,8,64,256]{3,2,1,0:T(8,128)}, u32[]{:S(2)}) copy-start(f32[4,8,64,256]{3,2,1,0:T(8,128)} %copy-done.12) | copy-start | bytes 6291460
  134.7 19.9 %collective-permute-start.13 = (f32[2,8,64,256]{3,2,1,0:T(8,128)S(1)}, f32[2,8,64,256]{3,2,1,0:T(8,128)S(1)}, u32[]{:S(2)}, u32[]{:S(2)}) collective-permute-start(f32[2,8,64,256]{3,2,1,0:T(8,128)S(1)} %slice_add_fusion), channel_id=1, source_target_pairs={{0,2},{1,5},{2,0},{3,7},{4,6},{5,1},{6,4},{7,3},{8,10},{9,13},{10,... | collective-permute-start | bytes 3145736 | tf_op jit(solution)/shard_map/ppermute | solution.py:325
  136.6 14.9 %collective-permute-start.12 = (f32[1,8,64,256]{3,2,1,0:T(8,128)S(1)}, f32[1,8,64,256]{3,2,1,0:T(8,128)S(1)}, u32[]{:S(2)}, u32[]{:S(2)}) collective-permute-start(f32[1,8,64,256]{3,2,1,0:T(8,128)S(1)} %slice_add_fusion.10), channel_id=1, source_target_pairs={{0,4},{1,3},{2,6},{3,1},{4,0},{5,7},{6,2},{7,5},{8,12},{9,11},{10,... | collective-permute-start | bytes 1572872 | tf_op jit(solution)/shard_map/ppermute | solution.py:325
  137.2 24.6 %collective-permute-start.9 = (f32[8,64,256]{2,1,0:T(8,128)S(1)}, f32[8,64,256]{2,1,0:T(8,128)S(1)}, u32[]{:S(2)}, u32[]{:S(2)}) collective-permute-start(f32[8,64,256]{2,1,0:T(8,128)S(1)} %bitcast.24), channel_id=1, source_target_pairs={{0,16},{8,24},{16,0},{24,8},{1,17},{9,25},{17,1},{25,9},{2,18},{10... | collective-permute-start | bytes 1572872 | tf_op jit(solution)/shard_map/ppermute | solution.py:329
  151.6 20.7 %collective-permute-start.15 = (f32[8,64,256]{2,1,0:T(8,128)S(1)}, f32[8,64,256]{2,1,0:T(8,128)S(1)}, u32[]{:S(2)}, u32[]{:S(2)}) collective-permute-start(f32[8,64,256]{2,1,0:T(8,128)S(1)} %bitcast.28), channel_id=1, source_target_pairs={{0,8},{8,0},{16,24},{24,16},{1,9},{9,1},{17,25},{25,17},{2,10},{10... | collective-permute-start | bytes 1572872 | tf_op jit(solution)/shard_map/ppermute | solution.py:329
  155.7 17.0 %collective-permute-start.17 = (f32[1,8,64,256]{3,2,1,0:T(8,128)S(1)}, f32[1,8,64,256]{3,2,1,0:T(8,128)S(1)}, u32[]{:S(2)}, u32[]{:S(2)}) collective-permute-start(f32[1,8,64,256]{3,2,1,0:T(8,128)S(1)} %slice_add_fusion.6.refs_0_), channel_id=1, source_target_pairs={{0,4},{1,3},{2,6},{3,1},{4,0},{5,7},{6,2},{7,5},{8,12},{9,11},{10,... | collective-permute-start | bytes 1572872 | tf_op jit(solution)/shard_map/ppermute | solution.py:325
  173.9 26.1 %collective-permute-start.18 = (f32[8,64,256]{2,1,0:T(8,128)S(1)}, f32[8,64,256]{2,1,0:T(8,128)S(1)}, u32[]{:S(2)}, u32[]{:S(2)}) collective-permute-start(f32[8,64,256]{2,1,0:T(8,128)S(1)} %bitcast.26), channel_id=1, source_target_pairs={{0,8},{8,0},{16,24},{24,16},{1,9},{9,1},{17,25},{25,17},{2,10},{10... | collective-permute-start | bytes 1572872 | tf_op jit(solution)/shard_map/ppermute | solution.py:329
  174.0 46.6 %collective-permute-start.8 = (f32[8,64,256]{2,1,0:T(8,128)S(1)}, f32[8,64,256]{2,1,0:T(8,128)S(1)}, u32[]{:S(2)}, u32[]{:S(2)}) collective-permute-start(f32[8,64,256]{2,1,0:T(8,128)S(1)} %get-tuple-element.52), channel_id=1, source_target_pairs={{0,8},{8,0},{16,24},{24,16},{1,9},{9,1},{17,25},{25,17},{2,10},{10... | collective-permute-start | bytes 1572872 | tf_op jit(solution)/shard_map/ppermute | solution.py:338
  176.0 54.3 %collective-permute-start.14 = (f32[8,64,256]{2,1,0:T(8,128)S(1)}, f32[8,64,256]{2,1,0:T(8,128)S(1)}, u32[]{:S(2)}, u32[]{:S(2)}) collective-permute-start(f32[8,64,256]{2,1,0:T(8,128)S(1)} %get-tuple-element.59.refs_0_), channel_id=1, source_target_pairs={{0,8},{8,0},{16,24},{24,16},{1,9},{9,1},{17,25},{25,17},{2,10},{10... | collective-permute-start | bytes 1572872 | tf_op jit(solution)/shard_map/ppermute | solution.py:338
  176.1 55.1 %collective-permute-start.16 = (f32[8,64,256]{2,1,0:T(8,128)S(1)}, f32[8,64,256]{2,1,0:T(8,128)S(1)}, u32[]{:S(2)}, u32[]{:S(2)}) collective-permute-start(f32[8,64,256]{2,1,0:T(8,128)S(1)} %get-tuple-element.61), channel_id=1, source_target_pairs={{0,16},{8,24},{16,0},{24,8},{1,17},{9,25},{17,1},{25,9},{2,18},{10... | collective-permute-start | bytes 1572872 | tf_op jit(solution)/shard_map/ppermute | solution.py:338
  200.5 34.3 %collective-permute-start.19 = (f32[8,64,256]{2,1,0:T(8,128)S(1)}, f32[8,64,256]{2,1,0:T(8,128)S(1)}, u32[]{:S(2)}, u32[]{:S(2)}) collective-permute-start(f32[8,64,256]{2,1,0:T(8,128)S(1)} %get-tuple-element.64), channel_id=1, source_target_pairs={{0,16},{8,24},{16,0},{24,8},{1,17},{9,25},{17,1},{25,9},{2,18},{10... | collective-permute-start | bytes 1572872 | tf_op jit(solution)/shard_map/ppermute | solution.py:338
  (4 other events, 3.7 us)
where the time goes:
time: 237 us; the launch traced here: 236 us
  waiting for transfers between devices  120 us (51%)
  Pallas kernels  85.1 us (36%)
  starting transfers between devices  18.7 us (8%)
  other arithmetic  8.06 us (3%)
  local copies, waits for them, and re-layouts  3.86 us (2%)
    pallas_call x3, Pallas kernels, spectra_of(): pl.pallas_call(functools.partial(spectral_kernel, scale=scale, classes=cl...  52.5 us
    ppermute x4, waiting for transfers between devices, added(): lax.ppermute(own, 'emit', [(z, z ^ gaps[cls]) for z in range(ne)])  48.5 us
    ppermute x8, waiting for transfers between devices, added(): arrived.append(lax.ppermute(total, 'elem', swaps[stage]))  39.3 us
    ppermute x4, waiting for transfers between devices, decoded(): lax.ppermute(part, 'emit', [(z, z ^ gap) for z in range(ne)])  31.7 us
    pallas_call x4, Pallas kernels, steer_blocks(): pl.pallas_call(functools.partial(steer_kernel, tokens=len(after)), grid_s...  27.4 us
    ppermute x8, starting transfers between devices, added(): arrived.append(lax.ppermute(total, 'elem', swaps[stage]))  10.2 us
    add x12, other arithmetic, added(): total = total + array[start:start + high - low]  6.93 us
  transfers between devices with their start and end apart: 20, of which 11 were waited for; matrix products, arithmetic and copies ran while one was open for 3% of the time, Pallas kernels for 19%

commit v1 on v0

--- a/solution.py
+++ b/solution.py
@@ -10,6 +10,7 @@
 
 
 ROWS = 8
+SLOTS = 3
 VMEM_LIMIT = 24 * 1024 * 1024
 ANY = pl.BlockSpec(memory_space=pl.ANY)
 
@@ -25,10 +26,11 @@
 
 
 def phase_table(samples, taps, freqs):
-    freqs = np.concatenate([freqs, freqs])
     inner = np.arange(taps)[:, None] * freqs[None, :] % samples * (2 * np.pi / samples)
     outer = np.arange(samples // taps)[:, None] * taps * freqs[None, :] % samples * (2 * np.pi / samples)
-    return np.concatenate([f(a).astype(np.float32) for a in (inner, outer) for f in (np.cos, np.sin)])
+    cosine, sine, wcos, wsin = np.cos(inner), np.sin(inner), np.cos(outer), np.sin(outer)
+    pairs = [(cosine, sine), (-sine, cosine), (cosine, cosine), (sine, sine), (wcos, wcos), (wsin, wsin)]
+    return np.concatenate([np.concatenate(pair, axis=1) for pair in pairs]).astype(np.float32)
 
 
 def folds(cls, nblock):
@@ -40,22 +42,23 @@
     return [(first, 0)] + [([(1, j)] + [(s, j + b) for s, b in first], j) for j in range(1, quarter)]
 
 
-def spectral_kernel(base_ref, code_ref, x_ref, codes_hbm, table_hbm, *refs, scale, classes, tokens):
+def spectral_kernel(base_ref, code_ref, codes_ref, table_ref, x_hbm, *refs, scale, classes, tokens):
     count = len(classes)
     refs = refs[tokens:]
-    outs, helds, (codes_ref, table_ref, sems) = refs[:count], refs[count : 2 * count], refs[2 * count :]
-    rows, mdev, samples = x_ref.shape
+    outs, helds, (x_ref, sems) = refs[:count], refs[count : 2 * count], refs[2 * count :]
+    slots, rows, mdev, samples = x_ref.shape
     ncode, _, taps = codes_ref.shape
     nblock = samples // taps
-    step = pl.program_id(0)
-
-    @pl.when(step == 0)
-    def _():
-        copies = [pltpu.make_async_copy(codes_hbm, codes_ref, sems.at[0]), pltpu.make_async_copy(table_hbm, table_ref, sems.at[1])]
-        for copy in copies:
-            copy.start()
-        for copy in copies:
-            copy.wait()
+    edev = x_hbm.shape[0]
+    steps = edev // rows
+
+    def fetch(step, slot):
+        return pltpu.make_async_copy(x_hbm.at[pl.ds(step * rows, rows)], x_ref.at[slot], sems.at[slot])
+
+    for step in range(min(slots, steps)):
+        fetch(step, step).start()
+
+    def tables():
         row = lax.broadcasted_iota(jnp.int32, (taps, taps), 0)
         col = lax.broadcasted_iota(jnp.int32, (taps, taps), 1)
         triangle = jnp.where(col <= row, 1.0, 0.0).astype(jnp.bfloat16)
@@ -64,51 +67,72 @@
             pair = codes_ref[code]
             ci, cq = (jnp.sum(jnp.where(row == col, pair[q : q + 1], 0.0), axis=1, keepdims=True) for q in (0, 1))
             for k, cls in enumerate(classes):
-                cosine, sine = table_ref[k, :taps], table_ref[k, taps : 2 * taps]
-                wcos_ref, wsin_ref = (table_ref.at[k, pl.ds(2 * taps + q * nblock, nblock)] for q in (0, 1))
+                first, second, cosine, sine = (table_ref[k, q * taps : (q + 1) * taps] for q in range(4))
+                wcos_ref, wsin_ref = (table_ref.at[k, pl.ds(4 * taps + q * nblock, nblock)] for q in (0, 1))
                 width = cosine.shape[1]
                 left = lax.broadcasted_iota(jnp.int32, (taps, width), 1) < width // 2
-                terms = split(jnp.concatenate([ci * cosine - cq * sine, ci * sine + cq * cosine], axis=1))
-                summed = (dot(triangle, terms[0]) + dot(triangle, terms[1])) * scale
-                pr, pi = summed[:, :width], summed[:, width:]
+                high, low = split(ci * first + cq * second)
+                summed = (dot(triangle, high) + dot(triangle, low)) * scale
+                turned = pltpu.roll(summed, width // 2, axis=1)
+                turned = jnp.where(left, turned, -turned)
                 sums = folds(cls, nblock)
-                depth = (1 + len(sums)) * taps
+                lead = (1 + len(sums)) // 2 * 2
 
                 def put(place, value):
-                    high, low = split(value)
-                    both = jnp.concatenate([high, low], axis=1)
+                    both = jnp.concatenate(split(value), axis=1)
                     helds[k][code, pl.ds(place * taps, taps), :] = both
-                    helds[k][code, pl.ds(depth + place * taps, taps), :] = both
-
-                put(0, jnp.where(left, cosine * pr + sine * pi, cosine * pi - sine * pr))
-                gr, gi = pr[taps - 1 :, :], pi[taps - 1 :, :]
-                br, bi = cosine * gr + sine * gi, cosine * gi - sine * gr
+                    if place == lead:
+                        helds[k][code, pl.ds((place + 1) * taps, taps), :] = both
+
+                put(0, cosine * summed + sine * turned)
+                end, turned_end = summed[taps - 1 :, :], turned[taps - 1 :, :]
+                whole, turned_whole = cosine * end + sine * turned_end, cosine * turned_end - sine * end
                 for place, (_, power) in enumerate(sums):
-                    wr, wi = wcos_ref[power : power + 1, :], wsin_ref[power : power + 1, :]
-                    put(1 + place, jnp.where(left, br * wr + bi * wi, bi * wr - br * wi))
+                    put(1 + place, whole * wcos_ref[power : power + 1, :] + turned_whole * wsin_ref[power : power + 1, :])
             return carry
 
         lax.fori_loop(0, ncode, build, 0)
 
-    for e in range(rows):
+    def emission(step, slot, e):
         code = code_ref[base_ref[0] + step * rows + e]
         for k, cls in enumerate(classes):
-            parts = [x_ref[e, :, :taps]]
+            parts = [x_ref[slot, e, :, :taps]]
             for terms, _ in folds(cls, nblock):
                 total = None
                 for sign, b in terms:
-                    block = x_ref[e, :, b * taps : (b + 1) * taps]
+                    block = x_ref[slot, e, :, b * taps : (b + 1) * taps]
                     if total is None:
                         total = block if sign > 0 else -block
                     else:
                         total = total + block if sign > 0 else total - block
                 parts.append(total)
             pairs = [split(p) for p in parts]
-            source = jnp.concatenate([h for h, _ in pairs] + [l for _, l in pairs], axis=1)
-            both = dot(source, helds[k][code])
-            width = both.shape[1] // 2
-            flat = outs[k].reshape(width * rows, mdev)
-            flat[pl.ds(e, width, stride=rows), :] = (both[:, :width] + both[:, width:]).T
+            lead = len(pairs) // 2 * 2
+            width = outs[k].shape[1]
+            source = jnp.concatenate(
+                [jnp.concatenate([p[q] for p in pairs[:lead]], axis=1) for q in (0, 1)], axis=0
+            )
+            both = dot(source, helds[k][code, : lead * taps])
+            both = both[:mdev] + both[mdev:]
+            if lead < len(pairs):
+                both = both + dot(jnp.concatenate(pairs[lead], axis=1), helds[k][code, lead * taps :])
+            flat = outs[k].reshape(steps * width * rows, mdev)
+            flat[pl.ds(step * (width * rows) + e, width, stride=rows), :] = (both[:, :width] + both[:, width:]).T
+
+    def work(step, carry):
+        slot = lax.rem(step, slots)
+        fetch(step, slot).wait()
+        for e in range(rows):
+            emission(step, slot, e)
+
+        @pl.when(step + slots < steps)
+        def _():
+            fetch(step + slots, slot).start()
+
+        return carry
+
+    tables()
+    lax.fori_loop(0, steps, work, 0)
 
 
 def spectra_of(traces, codes, code_of, base, classes, bins, scale, after):
@@ -118,76 +142,79 @@
     table = jnp.asarray(np.stack([phase_table(samples, taps, np.arange(cls, bins, 4) - bins // 2) for cls in classes]))
     width = 2 * (bins // 4)
 
-    hbm = pl.BlockSpec(memory_space=pltpu.HBM)
-    depths = [2 * (1 + len(folds(cls, samples // taps))) * taps for cls in classes]
+    chunks = [1 + len(folds(cls, samples // taps)) for cls in classes]
+    depths = [(n + n % 2) * taps for n in chunks]
+    vmem, smem = pl.BlockSpec(memory_space=pltpu.VMEM), pl.BlockSpec(memory_space=pltpu.SMEM)
     return pl.pallas_call(
         functools.partial(spectral_kernel, scale=scale, classes=classes, tokens=len(after)),
-        grid_spec=pltpu.PrefetchScalarGridSpec(
-            num_scalar_prefetch=2,
-            grid=(edev // rows,),
-            in_specs=[pl.BlockSpec((rows, mdev, samples), lambda i, *s: (i, 0, 0)), hbm, hbm] + [ANY] * len(after),
-            out_specs=[pl.BlockSpec((width, rows, mdev), lambda i, *s: (0, i, 0))] * len(classes),
-            scratch_shapes=[pltpu.VMEM((ncode, depth, 2 * width), jnp.bfloat16) for depth in depths]
-            + [pltpu.VMEM(codes.shape, jnp.float32), pltpu.VMEM(table.shape, jnp.float32), pltpu.SemaphoreType.DMA((2,))],
-        ),
-        out_shape=[jax.ShapeDtypeStruct((width, edev, mdev), jnp.float32)] * len(classes),
+        in_specs=[smem, smem, vmem, vmem, pl.BlockSpec(memory_space=pltpu.HBM)] + [ANY] * len(after),
+        out_specs=[vmem] * len(classes),
+        scratch_shapes=[pltpu.VMEM((ncode, depth, 2 * width), jnp.bfloat16) for depth in depths]
+        + [pltpu.VMEM((SLOTS, rows, mdev, samples), jnp.float32), pltpu.SemaphoreType.DMA((SLOTS,))],
+        out_shape=[jax.ShapeDtypeStruct((edev // rows, width, rows, mdev), jnp.float32)] * len(classes),
         compiler_params=pltpu.CompilerParams(vmem_limit_bytes=VMEM_LIMIT),
         cost_estimate=pl.CostEstimate(
-            flops=edev * mdev * sum(depths) * 2 * width * 2,
+            flops=edev * mdev * 2 * sum(depths) * 2 * width * 2,
             bytes_accessed=traces.size * 4 + len(classes) * width * edev * mdev * 4, transcendentals=0,
         ),
         name="spectral",
-    )(base, code_of, traces, codes, table, *after)
-
-
-def steer_kernel(target_ref, *refs, tokens):
-    spectra_refs, steer_refs = refs[:2], refs[2:4]
-    sent_ref, kept_ref = refs[4 + tokens :]
-    nb, _, width = steer_refs[0].shape
+    )(base, code_of, codes, table, traces, *after)
+
+
+def steer_kernel(target_ref, spectra_ref, steer_hbm, *refs, cls, tokens):
+    sent_ref, kept_ref, steer_ref, sems = refs[tokens:]
+    slots, nb, mdev, width = steer_ref.shape
+    count, _, edev, _ = sent_ref.shape
     half = width // 2
-    step, steps = pl.program_id(0), pl.num_programs(0)
+
+    def fetch(place, slot):
+        source = steer_hbm.at[pl.ds(target_ref[place] * nb, nb), cls]
+        return pltpu.make_async_copy(source, steer_ref.at[slot], sems.at[slot])
+
+    for place in range(min(slots, 2 * count)):
+        fetch(place, place).start()
 
     def complex_rows(w):
         return jnp.concatenate([w, jnp.concatenate([-w[:, half:], w[:, :half]], axis=1)], axis=0)
 
-    def compute(out_ref):
-        for k in range(2):
+    def run(out_ref, first):
+        def body(block, carry):
+            place = first + block
+            slot = lax.rem(place, slots)
+            fetch(place, slot).wait()
+            start = target_ref[place] * nb
             for i in range(nb):
-                wh, wl = split(steer_refs[k][i])
-                sh, sl = split(jnp.concatenate([spectra_refs[k][0, i], spectra_refs[k][1, i]], axis=1))
-                edev = sh.shape[0]
+                wh, wl = split(steer_ref[slot, i])
+                parts = [spectra_ref[:, q, start + i].reshape(edev, mdev) for q in (0, 1)]
+                sh, sl = split(jnp.concatenate(parts, axis=1))
                 both = dot(jnp.concatenate([sh, sl], axis=0), complex_rows(wh))
-                out_ref[k, i] = both[:edev] + both[edev:] + dot(sh, complex_rows(wl))
-
-    @pl.when(step < steps // 2)
-    def _():
-        compute(sent_ref)
-
-    @pl.when(step >= steps // 2)
-    def _():
-        compute(kept_ref)
+                out_ref[block, i] = both[:edev] + both[edev:] + dot(sh, complex_rows(wl))
+
+            @pl.when(place + slots < 2 * count)
+            def _():
+                fetch(place + slots, slot).start()
+
+            return carry
+
+        lax.fori_loop(0, count, body, 0)
+
+    run(sent_ref, 0)
+    run(kept_ref, count)
 
 
 def steer_blocks(targets, spectra, steer, cls, after):
     count = targets.shape[0] // 2
-    _, total, edev, mdev = spectra.shape
+    _, _, total, _, mdev = spectra.shape
+    edev = spectra.shape[0] * spectra.shape[3]
     nb = total // (2 * count)
     width = steer.shape[3]
-    edge = count // 2
     shape = jax.ShapeDtypeStruct((count, nb, edev, width), jnp.float32)
+    vmem, smem = pl.BlockSpec(memory_space=pltpu.VMEM), pl.BlockSpec(memory_space=pltpu.SMEM)
     return pl.pallas_call(
-        functools.partial(steer_kernel, tokens=len(after)),
-        grid_spec=pltpu.PrefetchScalarGridSpec(
-            num_scalar_prefetch=1,
-            grid=(count,),
-            in_specs=[pl.BlockSpec((2, nb, edev, mdev), lambda i, t, k=k: (0, t[2 * i + k], 0, 0)) for k in range(2)]
-            + [pl.BlockSpec((nb, None, mdev, width), lambda i, t, k=k: (t[2 * i + k], cls, 0, 0)) for k in range(2)]
-            + [ANY] * len(after),
-            out_specs=[
-                pl.BlockSpec((2, nb, edev, width), lambda i, t: (jnp.minimum(i, edge - 1), 0, 0, 0)),
-                pl.BlockSpec((2, nb, edev, width), lambda i, t: (jnp.maximum(i - edge, 0), 0, 0, 0)),
-            ],
-        ),
+        functools.partial(steer_kernel, cls=cls, tokens=len(after)),
+        in_specs=[smem, vmem, pl.BlockSpec(memory_space=pltpu.HBM)] + [ANY] * len(after),
+        out_specs=[vmem, vmem],
+        scratch_shapes=[pltpu.VMEM((4, nb, mdev, width), jnp.float32), pltpu.SemaphoreType.DMA((4,))],
         out_shape=[shape, shape],
         compiler_params=pltpu.CompilerParams(vmem_limit_bytes=VMEM_LIMIT),
         cost_estimate=pl.CostEstimate(
@@ -195,7 +222,7 @@
             bytes_accessed=4 * total * (2 * edev * mdev + mdev * width + edev * width), transcendentals=0,
         ),
         name="steer",
-    )(targets, spectra, spectra, steer, steer, *after)
+    )(targets, spectra, steer, *after)
 
 
 def decode_kernel(signs_ref, own_ref, near_ref, *refs, tokens):
@@ -299,7 +326,7 @@
         nonlocal last
         out = spectra_of(traces, codes, code_of, base, classes, bins, scale, last)
         for cls, spectra in zip(classes, out):
-            state[cls]["spectra"] = spectra.reshape(2, bins // 4, edev, mdev)
+            state[cls]["spectra"] = spectra.reshape(edev // ROWS, 2, bins // 4, ROWS, mdev)
         last = [out[0]]
 
     def steered(cls):
@@ -352,11 +379,11 @@
     more = range(nbit - 2)
     return [
         ("spectral", 2, 0), ("steer", 2), ("steer", 0), ("sum", 2),
-        ("spectral", 1), *(("sum", 2) for _ in more), ("sum", 0), ("steer", 1), ("sum", 2),
+        ("spectral", 1), *(("sum", 2) for _ in more), ("steer", 1), ("sum", 2), ("sum", 0),
         ("spectral", 3), *(("sum", 0) for _ in more), ("sum", 1), ("steer", 3), ("sum", 0),
-        ("decode", 2), ("sum", 3), *(("sum", 1) for _ in more), ("sum", 1), *(("sum", 3) for _ in more),
-        ("decode", 0), ("decode", 1), ("sum", 3), ("decode", 3),
-        ("finish", 2), ("finish", 0), ("finish", 1), ("finish", 3),
+        ("decode", 2), *(("sum", 1) for _ in more), ("sum", 3), ("sum", 1), *(("sum", 3) for _ in more), ("sum", 3),
+        ("decode", 1), ("decode", 3), ("decode", 0),
+        ("finish", 2), ("finish", 1), ("finish", 0), ("finish", 3),
     ]
 
 

time: 237 us -> 212 us (0.89)
  Pallas kernels: 85.1 us -> 66.7 us
  waiting for transfers between devices: 120 us -> 104 us
  starting transfers between devices: 18.7 us -> 29 us
    pallas_call x3, Pallas kernels: 52.5 us -> 37.3 us  [spectra_of(): pl.pallas_call(functools.partial(spectral_kernel, scale=scale, classes=cl...]
    ppermute x4, waiting for transfers between devices: 31.7 us -> 24.2 us  [decoded(): lax.ppermute(part, 'emit', [(z, z ^ gap) for z in range(ne)])]
    ppermute x4, starting transfers between devices: 3.39 us -> 8.94 us  [added(): lax.ppermute(own, 'emit', [(z, z ^ gaps[cls]) for z in range(ne)])]
    ppermute x4, waiting for transfers between devices: 48.5 us -> 43.6 us  [added(): lax.ppermute(own, 'emit', [(z, z ^ gaps[cls]) for z in range(ne)])]
    pallas_call x4, Pallas kernels: 27.4 us -> 24.4 us  [steer_blocks(): pl.pallas_call(functools.partial(steer_kernel, cls=cls, tokens=len(after)...]
    ppermute x8, waiting for transfers between devices: 39.3 us -> 36.3 us  [added(): arrived.append(lax.ppermute(total, 'elem', swaps[stage]))]
    ppermute x8, starting transfers between devices: 10.2 us -> 12.8 us  [added(): arrived.append(lax.ppermute(total, 'elem', swaps[stage]))]
  transfers between devices with their start and end apart: 20 -> 20, of which waited for: 11 -> 12; matrix products, arithmetic and copies ran while one was open for 3% -> 2% of each run, Pallas kernels for 19% -> 19%
where the time goes in v1:
time: 212 us
  waiting for transfers between devices  104 us (49%)
  Pallas kernels  66.7 us (31%)
  starting transfers between devices  29 us (14%)
  other arithmetic  7.31 us (3%)
  local copies, waits for them, and re-layouts  3.95 us (2%)
    ppermute x4, waiting for transfers between devices, added(): lax.ppermute(own, 'emit', [(z, z ^ gaps[cls]) for z in range(ne)])  43.6 us
    pallas_call x3, Pallas kernels, spectra_of(): pl.pallas_call(functools.partial(spectral_kernel, scale=scale, classes=cl...  37.3 us
    ppermute x8, waiting for transfers between devices, added(): arrived.append(lax.ppermute(total, 'elem', swaps[stage]))  36.3 us
    pallas_call x4, Pallas kernels, steer_blocks(): pl.pallas_call(functools.partial(steer_kernel, cls=cls, tokens=len(after)...  24.4 us
    ppermute x4, waiting for transfers between devices, decoded(): lax.ppermute(part, 'emit', [(z, z ^ gap) for z in range(ne)])  24.2 us
    ppermute x8, starting transfers between devices, added(): arrived.append(lax.ppermute(total, 'elem', swaps[stage]))  12.8 us
    ppermute x4, starting transfers between devices, added(): lax.ppermute(own, 'emit', [(z, z ^ gaps[cls]) for z in range(ne)])  8.94 us
    ppermute x4, starting transfers between devices, decoded(): lax.ppermute(part, 'emit', [(z, z ^ gap) for z in range(ne)])  6.29 us
  transfers between devices with their start and end apart: 20, of which 12 were waited for; matrix products, arithmetic and copies ran while one was open for 2% of the time, Pallas kernels for 19%

profile of v1, /device:TPU:0, one launch (start us, length us, event | category | flops | bytes accessed | tf_op | source)
XLA Modules:
  0.0 211.5 jit_solution(12885636576114209027)
XLA Ops:
  3.1 12.5 %spectral.3 = (f32[8,128,8,128]{3,2,1,0:T(8,128)S(1)}, f32[8,128,8,128]{3,2,1,0:T(8,128)S(1)}) custom-call(s32[1]{0:T(128)} %bitcast.2.base_ref, s32[256]{0:T(256)S(1)} %copy-done.10, f32[4,2,128]{2,1,0:T(2,128)S(1)} %copy-done.8, f32[2,528,128]{2,1,0:T(8,128)S(1)} %copy-done.5, f32[64,128,1024]{2,1,0:T(8,128)} %x_hbm.5), custom_call_target="tpu_custom_call" | custom-call | flops 8589934592 | bytes 41943040 | tf_op jit(solution)/shard_map/spectral/pallas_call | solution.py:148
  15.6 5.8 %steer.4 = (f32[4,8,64,256]{3,2,1,0:T(8,128)S(1)}, f32[4,8,64,256]{3,2,1,0:T(8,128)S(1)}) custom-call(s32[8]{0:T(128)S(1)} %fusion.4.target_ref, f32[8,2,64,8,128]{4,3,2,1,0:T(8,128)S(1)} %bitcast.16, f32[64,4,128,256]{3,2,1,0:T(8,128)} %bitcast.26, f32[8,128,8,128]{3,2,1,0:T(8,128)S(1)} %get-tuple-element.35.refs_0_), custom_call_target="tpu_custom_call" | custom-call | flops 1610612736 | bytes 16777216 | tf_op jit(solution)/shard_map/steer/pallas_call | solution.py:213
  22.0 5.8 %steer.5 = (f32[4,8,64,256]{3,2,1,0:T(8,128)S(1)}, f32[4,8,64,256]{3,2,1,0:T(8,128)S(1)}) custom-call(s32[8]{0:T(128)S(1)} %fusion.4.target_ref, f32[8,2,64,8,128]{4,3,2,1,0:T(8,128)S(1)} %bitcast.21, f32[64,4,128,256]{3,2,1,0:T(8,128)} %bitcast.27, f32[4,8,64,256]{3,2,1,0:T(8,128)S(1)} %get-tuple-element.38.refs_0_), custom_call_target="tpu_custom_call" | custom-call | flops 1610612736 | bytes 16777216 | tf_op jit(solution)/shard_map/steer/pallas_call | solution.py:213
  28.0 2.6 %collective-permute-start.1 = (f32[2,8,64,256]{3,2,1,0:T(8,128)S(1)}, f32[2,8,64,256]{3,2,1,0:T(8,128)S(1)}, u32[]{:S(2)}, u32[]{:S(2)}) collective-permute-start(f32[2,8,64,256]{3,2,1,0:T(8,128)S(1)} %slice_add_fusion.3.refs_0_), channel_id=1, source_target_pairs={{0,2},{1,5},{2,0},{3,7},{4,6},{5,1},{6,4},{7,3},{8,10},{9,13},{10,... | collective-permute-start | bytes 3145736 | tf_op jit(solution)/shard_map/ppermute | solution.py:352
  30.8 12.4 %spectral.4 = f32[8,128,8,128]{3,2,1,0:T(8,128)S(1)} custom-call(s32[1]{0:T(128)} %bitcast.2.base_ref, s32[256]{0:T(256)S(1)} %copy-done.11, f32[4,2,128]{2,1,0:T(2,128)S(1)} %copy-done.9, f32[1,528,128]{2,1,0:T(8,128)S(1)} %copy-done.7, f32[64,128,1024]{2,1,0:T(8,128)} %x_hbm.5, f32[2,8,64,256]{3,2,1,0:T(8,128)S(1)} %slice_add_fusion.3.refs_0_), custom_call_target="tpu_custom_call" | custom-call | flops 6442450944 | bytes 37748736 | tf_op jit(solution)/shard_map/spectral/pallas_call | solution.py:148
  43.5 2.1 collective-permute-start.2
  45.6 5.8 %steer.6 = (f32[4,8,64,256]{3,2,1,0:T(8,128)S(1)}, f32[4,8,64,256]{3,2,1,0:T(8,128)S(1)}) custom-call(s32[8]{0:T(128)S(1)} %fusion.4.target_ref, f32[8,2,64,8,128]{4,3,2,1,0:T(8,128)S(1)} %bitcast.15, f32[64,4,128,256]{3,2,1,0:T(8,128)} %bitcast.28, f32[1,8,64,256]{3,2,1,0:T(8,128)S(1)} %slice_add_fusion.18.refs_0_), custom_call_target="tpu_custom_call" | custom-call | flops 1610612736 | bytes 16777216 | tf_op jit(solution)/shard_map/steer/pallas_call | solution.py:213
  51.4 1.3 collective-permute-done.2
  53.1 2.1 collective-permute-start.5
  55.2 12.4 %spectral.5 = f32[8,128,8,128]{3,2,1,0:T(8,128)S(1)} custom-call(s32[1]{0:T(128)} %bitcast.2.base_ref, s32[256]{0:T(256)S(1)} %copy-done.11, f32[4,2,128]{2,1,0:T(2,128)S(1)} %copy-done.9, f32[1,528,128]{2,1,0:T(8,128)S(1)} %copy-done.6, f32[64,128,1024]{2,1,0:T(8,128)} %x_hbm.5, f32[2,8,64,256]{3,2,1,0:T(8,128)S(1)} %slice_add_fusion.2.refs_0_), custom_call_target="tpu_custom_call" | custom-call | flops 6442450944 | bytes 37748736 | tf_op jit(solution)/shard_map/spectral/pallas_call | solution.py:148
  68.3 7.0 %steer.7 = (f32[4,8,64,256]{3,2,1,0:T(8,128)}, f32[4,8,64,256]{3,2,1,0:T(8,128)S(1)}) custom-call(s32[8]{0:T(128)S(1)} %fusion.4.target_ref, f32[8,2,64,8,128]{4,3,2,1,0:T(8,128)S(1)} %bitcast.14, f32[64,4,128,256]{3,2,1,0:T(8,128)} %bitcast.29, f32[2,8,64,256]{3,2,1,0:T(8,128)S(1)} %slice_add_fusion.1.refs_0_), custom_call_target="tpu_custom_call" | custom-call | flops 1610612736 | bytes 16777216 | tf_op jit(solution)/shard_map/steer/pallas_call | solution.py:213
  75.4 1.4 copy-done.3
  76.8 2.0 collective-permute-start.9
  78.9 1.5 collective-permute-start.7
  80.5 2.6 %collective-permute-start.3 = (f32[8,64,256]{2,1,0:T(8,128)S(1)}, f32[8,64,256]{2,1,0:T(8,128)S(1)}, u32[]{:S(2)}, u32[]{:S(2)}) collective-permute-start(f32[8,64,256]{2,1,0:T(8,128)S(1)} %bitcast.22), channel_id=1, source_target_pairs={{0,16},{8,24},{16,0},{24,8},{1,17},{9,25},{17,1},{25,9},{2,18},{10... | collective-permute-start | bytes 1572872 | tf_op jit(solution)/shard_map/ppermute | solution.py:356
  83.3 10.4 %collective-permute-done.7 = f32[1,8,64,256]{3,2,1,0:T(8,128)S(1)} collective-permute-done((f32[1,8,64,256]{3,2,1,0:T(8,128)S(1)}, f32[1,8,64,256]{3,2,1,0:T(8,128)S(1)}, u32[]{:S(2)}, u32[]{:S(2)}) %collective-permute-start.7) | collective-permute-done | bytes 524320 | tf_op jit(solution)/shard_map/ppermute | solution.py:352
  93.7 1.3 fusion.2.refs_0_
  95.1 11.3 %collective-permute-done.3.near_ref = f32[8,64,256]{2,1,0:T(8,128)S(1)} collective-permute-done((f32[8,64,256]{2,1,0:T(8,128)S(1)}, f32[8,64,256]{2,1,0:T(8,128)S(1)}, u32[]{:S(2)}, u32[]{:S(2)}) %collective-permute-start.3) | collective-permute-done | bytes 524320 | tf_op jit(solution)/shard_map/ppermute | solution.py:356
  107.0 1.4 slice_add_fusion
  109.4 14.4 %collective-permute-done.11 = f32[1,8,64,256]{3,2,1,0:T(8,128)S(1)} collective-permute-done((f32[1,8,64,256]{3,2,1,0:T(8,128)S(1)}, f32[1,8,64,256]{3,2,1,0:T(8,128)S(1)}, u32[]{:S(2)}, u32[]{:S(2)}) %collective-permute-start.11) | collective-permute-done | bytes 524320 | tf_op jit(solution)/shard_map/ppermute | solution.py:352
  123.9 3.3 %collective-permute-done.13 = f32[2,8,64,256]{3,2,1,0:T(8,128)S(1)} collective-permute-done((f32[2,8,64,256]{3,2,1,0:T(8,128)S(1)}, f32[2,8,64,256]{3,2,1,0:T(8,128)S(1)}, u32[]{:S(2)}, u32[]{:S(2)}) %collective-permute-start.13) | collective-permute-done | bytes 1048608 | tf_op jit(solution)/shard_map/ppermute | solution.py:352
  128.4 1.6 collective-permute-start.14
  129.9 1.3 collective-permute-start.12
  131.3 6.4 %collective-permute-done.14 = f32[1,8,64,256]{3,2,1,0:T(8,128)S(1)} collective-permute-done((f32[1,8,64,256]{3,2,1,0:T(8,128)S(1)}, f32[1,8,64,256]{3,2,1,0:T(8,128)S(1)}, u32[]{:S(2)}, u32[]{:S(2)}) %collective-permute-start.14) | collective-permute-done | bytes 524320 | tf_op jit(solution)/shard_map/ppermute | solution.py:352
  138.8 1.6 collective-permute-start.17
  140.5 3.4 %collective-permute-start.16 = (f32[8,64,256]{2,1,0:T(8,128)S(1)}, f32[8,64,256]{2,1,0:T(8,128)S(1)}, u32[]{:S(2)}, u32[]{:S(2)}) collective-permute-start(f32[8,64,256]{2,1,0:T(8,128)S(1)} %bitcast.17), channel_id=1, source_target_pairs={{0,16},{8,24},{16,0},{24,8},{1,17},{9,25},{17,1},{25,9},{2,18},{10... | collective-permute-start | bytes 1572872 | tf_op jit(solution)/shard_map/ppermute | solution.py:356
  144.1 12.1 %collective-permute-done.12.near_ref = f32[8,64,256]{2,1,0:T(8,128)S(1)} collective-permute-done((f32[8,64,256]{2,1,0:T(8,128)S(1)}, f32[8,64,256]{2,1,0:T(8,128)S(1)}, u32[]{:S(2)}, u32[]{:S(2)}) %collective-permute-start.12) | collective-permute-done | bytes 524320 | tf_op jit(solution)/shard_map/ppermute | solution.py:356
  156.7 1.8 collective-permute-start.15
  158.5 20.2 %collective-permute-done.17.near_ref = f32[8,64,256]{2,1,0:T(8,128)S(1)} collective-permute-done((f32[8,64,256]{2,1,0:T(8,128)S(1)}, f32[8,64,256]{2,1,0:T(8,128)S(1)}, u32[]{:S(2)}, u32[]{:S(2)}) %collective-permute-start.17) | collective-permute-done | bytes 524320 | tf_op jit(solution)/shard_map/ppermute | solution.py:356
  179.7 4.3 %collective-permute-start.19 = (f32[8,64,256]{2,1,0:T(8,128)S(1)}, f32[8,64,256]{2,1,0:T(8,128)S(1)}, u32[]{:S(2)}, u32[]{:S(2)}) collective-permute-start(f32[8,64,256]{2,1,0:T(8,128)S(1)} %get-tuple-element.61.refs_0_), channel_id=1, source_target_pairs={{0,16},{8,24},{16,0},{24,8},{1,17},{9,25},{17,1},{25,9},{2,18},{10... | collective-permute-start | bytes 1572872 | tf_op jit(solution)/shard_map/ppermute | solution.py:365
  183.9 16.6 %collective-permute-done.8.refs_1_ = f32[8,64,256]{2,1,0:T(8,128)S(1)} collective-permute-done((f32[8,64,256]{2,1,0:T(8,128)S(1)}, f32[8,64,256]{2,1,0:T(8,128)S(1)}, u32[]{:S(2)}, u32[]{:S(2)}) %collective-permute-start.8) | collective-permute-done | bytes 524320 | tf_op jit(solution)/shard_map/ppermute | solution.py:365
  202.2 7.6 %collective-permute-done.18.refs_2_ = f32[8,64,256]{2,1,0:T(8,128)S(1)} collective-permute-done((f32[8,64,256]{2,1,0:T(8,128)S(1)}, f32[8,64,256]{2,1,0:T(8,128)S(1)}, u32[]{:S(2)}, u32[]{:S(2)}) %collective-permute-start.18) | collective-permute-done | bytes 524320 | tf_op jit(solution)/shard_map/ppermute | solution.py:365
  (75 shorter events, 15.0 us)
Async XLA Ops:
  21.4 6.4 %collective-permute-start = (f32[4,8,64,256]{3,2,1,0:T(8,128)S(1)}, f32[4,8,64,256]{3,2,1,0:T(8,128)S(1)}, u32[]{:S(2)}, u32[]{:S(2)}) collective-permute-start(f32[4,8,64,256]{3,2,1,0:T(8,128)S(1)} %get-tuple-element.38.refs_0_), channel_id=1, source_target_pairs={{0,1},{1,0},{2,3},{3,2},{4,5},{5,4},{6,7},{7,6},{8,9},{9,8},{10,11... | collective-permute-start | bytes 6291464 | tf_op jit(solution)/shard_map/ppermute | solution.py:337
  27.7 40.3 %copy-start.2 = (f32[4,8,64,256]{3,2,1,0:T(8,128)}, f32[4,8,64,256]{3,2,1,0:T(8,128)S(1)}, u32[]{:S(2)}) copy-start(f32[4,8,64,256]{3,2,1,0:T(8,128)S(1)} %get-tuple-element.50) | copy-start | bytes 6291460
  27.8 3.1 %copy-start.7 = (f32[1,528,128]{2,1,0:T(8,128)S(1)}, f32[1,528,128]{2,1,0:T(8,128)}, u32[]{:S(2)}) copy-start(f32[1,528,128]{2,1,0:T(8,128)} %constant.34.clone.table_ref) | copy-start | bytes 811012
  27.8 3.1 %copy-start.9 = (f32[4,2,128]{2,1,0:T(2,128)S(1)}, f32[4,2,128]{2,1,0:T(2,128)}, u32[]{:S(2)}) copy-start(f32[4,2,128]{2,1,0:T(2,128)} %codes_ref.5) | copy-start | bytes 12292
  27.8 3.0 %copy-start.11 = (s32[256]{0:T(256)S(1)}, s32[256]{0:T(256)}, u32[]{:S(2)}) copy-start(s32[256]{0:T(256)} %code_ref.5) | copy-start | bytes 3076
  28.0 15.3 %collective-permute-start.1 = (f32[2,8,64,256]{3,2,1,0:T(8,128)S(1)}, f32[2,8,64,256]{3,2,1,0:T(8,128)S(1)}, u32[]{:S(2)}, u32[]{:S(2)}) collective-permute-start(f32[2,8,64,256]{3,2,1,0:T(8,128)S(1)} %slice_add_fusion.3.refs_0_), channel_id=1, source_target_pairs={{0,2},{1,5},{2,0},{3,7},{4,6},{5,1},{6,4},{7,3},{8,10},{9,13},{10,... | collective-permute-start | bytes 3145736 | tf_op jit(solution)/shard_map/ppermute | solution.py:352
  30.6 22.3 %collective-permute-start.4 = (f32[4,8,64,256]{3,2,1,0:T(8,128)S(1)}, f32[4,8,64,256]{3,2,1,0:T(8,128)S(1)}, u32[]{:S(2)}, u32[]{:S(2)}) collective-permute-start(f32[4,8,64,256]{3,2,1,0:T(8,128)S(1)} %get-tuple-element.39), channel_id=1, source_target_pairs={{0,1},{1,0},{2,3},{3,2},{4,5},{5,4},{6,7},{7,6},{8,9},{9,8},{10,11... | collective-permute-start | bytes 6291464 | tf_op jit(solution)/shard_map/ppermute | solution.py:337
  43.5 9.3 %collective-permute-start.2 = (f32[1,8,64,256]{3,2,1,0:T(8,128)S(1)}, f32[1,8,64,256]{3,2,1,0:T(8,128)S(1)}, u32[]{:S(2)}, u32[]{:S(2)}) collective-permute-start(f32[1,8,64,256]{3,2,1,0:T(8,128)S(1)} %slice_add_fusion.18.refs_0_), channel_id=1, source_target_pairs={{0,4},{1,3},{2,6},{3,1},{4,0},{5,7},{6,2},{7,5},{8,12},{9,11},{10,... | collective-permute-start | bytes 1572872 | tf_op jit(solution)/shard_map/ppermute | solution.py:352
  51.4 16.8 %copy-start = (f32[4,8,64,256]{3,2,1,0:T(8,128)}, f32[4,8,64,256]{3,2,1,0:T(8,128)S(1)}, u32[]{:S(2)}) copy-start(f32[4,8,64,256]{3,2,1,0:T(8,128)S(1)} %get-tuple-element.56) | copy-start | bytes 6291460
  51.4 16.7 %collective-permute-start.6 = (f32[4,8,64,256]{3,2,1,0:T(8,128)S(1)}, f32[4,8,64,256]{3,2,1,0:T(8,128)S(1)}, u32[]{:S(2)}, u32[]{:S(2)}) collective-permute-start(f32[4,8,64,256]{3,2,1,0:T(8,128)S(1)} %get-tuple-element.42), channel_id=1, source_target_pairs={{0,1},{1,0},{2,3},{3,2},{4,5},{5,4},{6,7},{7,6},{8,9},{9,8},{10,11... | collective-permute-start | bytes 6291464 | tf_op jit(solution)/shard_map/ppermute | solution.py:337
  52.9 2.3 %copy-start.6 = (f32[1,528,128]{2,1,0:T(8,128)S(1)}, f32[1,528,128]{2,1,0:T(8,128)}, u32[]{:S(2)}) copy-start(f32[1,528,128]{2,1,0:T(8,128)} %constant.35.clone.table_ref) | copy-start | bytes 811012
  52.9 15.1 %copy-start.14 = (f32[4,8,64,256]{3,2,1,0:T(8,128)}, f32[4,8,64,256]{3,2,1,0:T(8,128)S(1)}, u32[]{:S(2)}) copy-start(f32[4,8,64,256]{3,2,1,0:T(8,128)S(1)} %collective-permute-done.4) | copy-start | bytes 6291460
  53.1 14.9 %collective-permute-start.5 = (f32[2,8,64,256]{3,2,1,0:T(8,128)S(1)}, f32[2,8,64,256]{3,2,1,0:T(8,128)S(1)}, u32[]{:S(2)}, u32[]{:S(2)}) collective-permute-start(f32[2,8,64,256]{3,2,1,0:T(8,128)S(1)} %slice_add_fusion.2.refs_0_), channel_id=1, source_target_pairs={{0,2},{1,5},{2,0},{3,7},{4,6},{5,1},{6,4},{7,3},{8,10},{9,13},{10,... | collective-permute-start | bytes 3145736 | tf_op jit(solution)/shard_map/ppermute | solution.py:352
  68.1 7.2 %copy-start.12 = (f32[4,8,64,256]{3,2,1,0:T(8,128)}, f32[4,8,64,256]{3,2,1,0:T(8,128)S(1)}, u32[]{:S(2)}) copy-start(f32[4,8,64,256]{3,2,1,0:T(8,128)S(1)} %collective-permute-done.6) | copy-start | bytes 6291460
  68.3 10.5 %copy-start.15 = (s32[256]{0:T(256)S(1)}, s32[256]{0:T(256)}, u32[]{:S(2)}) copy-start(s32[256]{0:T(256)} %param.13) | copy-start | bytes 3076
  76.8 30.2 %collective-permute-start.10 = (f32[4,8,64,256]{3,2,1,0:T(8,128)}, f32[4,8,64,256]{3,2,1,0:T(8,128)}, u32[]{:S(2)}, u32[]{:S(2)}) collective-permute-start(f32[4,8,64,256]{3,2,1,0:T(8,128)} %get-tuple-element.49), channel_id=1, source_target_pairs={{0,1},{1,0},{2,3},{3,2},{4,5},{5,4},{6,7},{7,6},{8,9},{9,8},{10,11... | collective-permute-start | bytes 6291464 | tf_op jit(solution)/shard_map/ppermute | solution.py:337
  76.8 30.1 %collective-permute-start.9 = (f32[2,8,64,256]{3,2,1,0:T(8,128)S(1)}, f32[2,8,64,256]{3,2,1,0:T(8,128)S(1)}, u32[]{:S(2)}, u32[]{:S(2)}) collective-permute-start(f32[2,8,64,256]{3,2,1,0:T(8,128)S(1)} %slice_add_fusion.1.refs_0_), channel_id=1, source_target_pairs={{0,2},{1,5},{2,0},{3,7},{4,6},{5,1},{6,4},{7,3},{8,10},{9,13},{10,... | collective-permute-start | bytes 3145736 | tf_op jit(solution)/shard_map/ppermute | solution.py:352
  78.9 14.8 %collective-permute-start.7 = (f32[1,8,64,256]{3,2,1,0:T(8,128)S(1)}, f32[1,8,64,256]{3,2,1,0:T(8,128)S(1)}, u32[]{:S(2)}, u32[]{:S(2)}) collective-permute-start(f32[1,8,64,256]{3,2,1,0:T(8,128)S(1)} %slice_add_fusion.14), channel_id=1, source_target_pairs={{0,4},{1,3},{2,6},{3,1},{4,0},{5,7},{6,2},{7,5},{8,12},{9,11},{10,... | collective-permute-start | bytes 1572872 | tf_op jit(solution)/shard_map/ppermute | solution.py:352
  80.5 25.9 %collective-permute-start.3 = (f32[8,64,256]{2,1,0:T(8,128)S(1)}, f32[8,64,256]{2,1,0:T(8,128)S(1)}, u32[]{:S(2)}, u32[]{:S(2)}) collective-permute-start(f32[8,64,256]{2,1,0:T(8,128)S(1)} %bitcast.22), channel_id=1, source_target_pairs={{0,16},{8,24},{16,0},{24,8},{1,17},{9,25},{17,1},{25,9},{2,18},{10... | collective-permute-start | bytes 1572872 | tf_op jit(solution)/shard_map/ppermute | solution.py:356
  83.3 23.6 %copy-start.1 = (f32[4,8,64,256]{3,2,1,0:T(8,128)S(1)}, f32[4,8,64,256]{3,2,1,0:T(8,128)}, u32[]{:S(2)}) copy-start(f32[4,8,64,256]{3,2,1,0:T(8,128)} %copy-done) | copy-start | bytes 6291460
  83.3 23.6 %copy-start.13 = (f32[4,8,64,256]{3,2,1,0:T(8,128)S(1)}, f32[4,8,64,256]{3,2,1,0:T(8,128)}, u32[]{:S(2)}) copy-start(f32[4,8,64,256]{3,2,1,0:T(8,128)} %copy-done.12) | copy-start | bytes 6291460
  95.1 11.9 %copy-start.4 = (f32[4,8,64,256]{3,2,1,0:T(8,128)S(1)}, f32[4,8,64,256]{3,2,1,0:T(8,128)}, u32[]{:S(2)}) copy-start(f32[4,8,64,256]{3,2,1,0:T(8,128)} %copy-done.3) | copy-start | bytes 6291460
  108.4 18.9 %collective-permute-start.13 = (f32[2,8,64,256]{3,2,1,0:T(8,128)S(1)}, f32[2,8,64,256]{3,2,1,0:T(8,128)S(1)}, u32[]{:S(2)}, u32[]{:S(2)}) collective-permute-start(f32[2,8,64,256]{3,2,1,0:T(8,128)S(1)} %slice_add_fusion), channel_id=1, source_target_pairs={{0,2},{1,5},{2,0},{3,7},{4,6},{5,1},{6,4},{7,3},{8,10},{9,13},{10,... | collective-permute-start | bytes 3145736 | tf_op jit(solution)/shard_map/ppermute | solution.py:352
  109.0 14.8 %collective-permute-start.11 = (f32[1,8,64,256]{3,2,1,0:T(8,128)S(1)}, f32[1,8,64,256]{3,2,1,0:T(8,128)S(1)}, u32[]{:S(2)}, u32[]{:S(2)}) collective-permute-start(f32[1,8,64,256]{3,2,1,0:T(8,128)S(1)} %slice_add_fusion.10), channel_id=1, source_target_pairs={{0,4},{1,3},{2,6},{3,1},{4,0},{5,7},{6,2},{7,5},{8,12},{9,11},{10,... | collective-permute-start | bytes 1572872 | tf_op jit(solution)/shard_map/ppermute | solution.py:352
  128.4 9.2 %collective-permute-start.14 = (f32[1,8,64,256]{3,2,1,0:T(8,128)S(1)}, f32[1,8,64,256]{3,2,1,0:T(8,128)S(1)}, u32[]{:S(2)}, u32[]{:S(2)}) collective-permute-start(f32[1,8,64,256]{3,2,1,0:T(8,128)S(1)} %slice_add_fusion.6), channel_id=1, source_target_pairs={{0,4},{1,3},{2,6},{3,1},{4,0},{5,7},{6,2},{7,5},{8,12},{9,11},{10,... | collective-permute-start | bytes 1572872 | tf_op jit(solution)/shard_map/ppermute | solution.py:352
  129.9 26.3 %collective-permute-start.12 = (f32[8,64,256]{2,1,0:T(8,128)S(1)}, f32[8,64,256]{2,1,0:T(8,128)S(1)}, u32[]{:S(2)}, u32[]{:S(2)}) collective-permute-start(f32[8,64,256]{2,1,0:T(8,128)S(1)} %bitcast.24), channel_id=1, source_target_pairs={{0,8},{8,0},{16,24},{24,16},{1,9},{9,1},{17,25},{25,17},{2,10},{10... | collective-permute-start | bytes 1572872 | tf_op jit(solution)/shard_map/ppermute | solution.py:356
  138.8 39.9 %collective-permute-start.17 = (f32[8,64,256]{2,1,0:T(8,128)S(1)}, f32[8,64,256]{2,1,0:T(8,128)S(1)}, u32[]{:S(2)}, u32[]{:S(2)}) collective-permute-start(f32[8,64,256]{2,1,0:T(8,128)S(1)} %bitcast.19), channel_id=1, source_target_pairs={{0,8},{8,0},{16,24},{24,16},{1,9},{9,1},{17,25},{25,17},{2,10},{10... | collective-permute-start | bytes 1572872 | tf_op jit(solution)/shard_map/ppermute | solution.py:356
  140.5 38.7 %collective-permute-start.16 = (f32[8,64,256]{2,1,0:T(8,128)S(1)}, f32[8,64,256]{2,1,0:T(8,128)S(1)}, u32[]{:S(2)}, u32[]{:S(2)}) collective-permute-start(f32[8,64,256]{2,1,0:T(8,128)S(1)} %bitcast.17), channel_id=1, source_target_pairs={{0,16},{8,24},{16,0},{24,8},{1,17},{9,25},{17,1},{25,9},{2,18},{10... | collective-permute-start | bytes 1572872 | tf_op jit(solution)/shard_map/ppermute | solution.py:356
  144.0 56.5 %collective-permute-start.8 = (f32[8,64,256]{2,1,0:T(8,128)S(1)}, f32[8,64,256]{2,1,0:T(8,128)S(1)}, u32[]{:S(2)}, u32[]{:S(2)}) collective-permute-start(f32[8,64,256]{2,1,0:T(8,128)S(1)} %get-tuple-element.52), channel_id=1, source_target_pairs={{0,8},{8,0},{16,24},{24,16},{1,9},{9,1},{17,25},{25,17},{2,10},{10... | collective-permute-start | bytes 1572872 | tf_op jit(solution)/shard_map/ppermute | solution.py:365
  156.7 44.7 %collective-permute-start.15 = (f32[8,64,256]{2,1,0:T(8,128)S(1)}, f32[8,64,256]{2,1,0:T(8,128)S(1)}, u32[]{:S(2)}, u32[]{:S(2)}) collective-permute-start(f32[8,64,256]{2,1,0:T(8,128)S(1)} %get-tuple-element.60.refs_0_), channel_id=1, source_target_pairs={{0,16},{8,24},{16,0},{24,8},{1,17},{9,25},{17,1},{25,9},{2,18},{10... | collective-permute-start | bytes 1572872 | tf_op jit(solution)/shard_map/ppermute | solution.py:365
  179.6 30.3 %collective-permute-start.18 = (f32[8,64,256]{2,1,0:T(8,128)S(1)}, f32[8,64,256]{2,1,0:T(8,128)S(1)}, u32[]{:S(2)}, u32[]{:S(2)}) collective-permute-start(f32[8,64,256]{2,1,0:T(8,128)S(1)} %get-tuple-element.63), channel_id=1, source_target_pairs={{0,8},{8,0},{16,24},{24,16},{1,9},{9,1},{17,25},{25,17},{2,10},{10... | collective-permute-start | bytes 1572872 | tf_op jit(solution)/shard_map/ppermute | solution.py:365
  179.7 31.0 %collective-permute-start.19 = (f32[8,64,256]{2,1,0:T(8,128)S(1)}, f32[8,64,256]{2,1,0:T(8,128)S(1)}, u32[]{:S(2)}, u32[]{:S(2)}) collective-permute-start(f32[8,64,256]{2,1,0:T(8,128)S(1)} %get-tuple-element.61.refs_0_), channel_id=1, source_target_pairs={{0,16},{8,24},{16,0},{24,8},{1,17},{9,25},{17,1},{25,9},{2,18},{10... | collective-permute-start | bytes 1572872 | tf_op jit(solution)/shard_map/ppermute | solution.py:365
  (4 other events, 3.8 us)

commit v2 on v1

--- a/solution.py
+++ b/solution.py
@@ -12,6 +12,7 @@
 ROWS = 8
 SLOTS = 3
 VMEM_LIMIT = 24 * 1024 * 1024
+STEER_VMEM_LIMIT = 32 * 1024 * 1024
 ANY = pl.BlockSpec(memory_space=pl.ANY)
 
 
@@ -216,7 +217,7 @@
         out_specs=[vmem, vmem],
         scratch_shapes=[pltpu.VMEM((4, nb, mdev, width), jnp.float32), pltpu.SemaphoreType.DMA((4,))],
         out_shape=[shape, shape],
-        compiler_params=pltpu.CompilerParams(vmem_limit_bytes=VMEM_LIMIT),
+        compiler_params=pltpu.CompilerParams(vmem_limit_bytes=STEER_VMEM_LIMIT),
         cost_estimate=pl.CostEstimate(
             flops=total * edev * 2 * mdev * width * 2 * 3,
             bytes_accessed=4 * total * (2 * edev * mdev + mdev * width + edev * width), transcendentals=0,
@@ -379,10 +380,10 @@
     more = range(nbit - 2)
     return [
         ("spectral", 2, 0), ("steer", 2), ("steer", 0), ("sum", 2),
-        ("spectral", 1), *(("sum", 2) for _ in more), ("steer", 1), ("sum", 2), ("sum", 0),
-        ("spectral", 3), *(("sum", 0) for _ in more), ("sum", 1), ("steer", 3), ("sum", 0),
-        ("decode", 2), *(("sum", 1) for _ in more), ("sum", 3), ("sum", 1), *(("sum", 3) for _ in more), ("sum", 3),
-        ("decode", 1), ("decode", 3), ("decode", 0),
+        ("spectral", 1), *(("sum", 2) for _ in more), ("steer", 1), ("sum", 2), ("sum", 0), ("sum", 1),
+        ("spectral", 3), ("steer", 3), *(("sum", 0) for _ in more), *(("sum", 1) for _ in more), ("decode", 2),
+        ("sum", 0), ("sum", 3), ("sum", 1), *(("sum", 3) for _ in more), ("decode", 1), ("sum", 3),
+        ("decode", 3), ("decode", 0),
         ("finish", 2), ("finish", 1), ("finish", 0), ("finish", 3),
     ]
 

time: 212 us -> 219 us (1.033)
  waiting for transfers between devices: 104 us -> 111 us
  starting transfers between devices: 29 us -> 23.5 us
  other arithmetic: 7.31 us -> 10.8 us
    ppermute x4, waiting for transfers between devices: 24.2 us -> 37.1 us  [decoded(): lax.ppermute(part, 'emit', [(z, z ^ gap) for z in range(ne)])]
    ppermute x4, waiting for transfers between devices: 43.6 us -> 35.3 us  [added(): lax.ppermute(own, 'emit', [(z, z ^ gaps[cls]) for z in range(ne)])]
    add x12, other arithmetic: 6.18 us -> 9.66 us  [added(): total = total + array[start:start + high - low]]
    ppermute x8, waiting for transfers between devices: 36.3 us -> 39.1 us  [added(): arrived.append(lax.ppermute(total, 'elem', swaps[stage]))]
    ppermute x4, starting transfers between devices: 6.29 us -> 3.85 us  [decoded(): lax.ppermute(part, 'emit', [(z, z ^ gap) for z in range(ne)])]
    unnamed x32 -> x30, local copies, waits for them, and re-layouts: 3.87 us -> 5.17 us
  transfers between devices with their start and end apart: 20 -> 20, of which waited for: 12 -> 14; matrix products, arithmetic and copies ran while one was open for 2% -> 3% of each run, Pallas kernels for 19% -> 22%
where the time goes in v2:
time: 219 us; the launch traced here: 218 us
  waiting for transfers between devices  111 us (51%)
  Pallas kernels  66.6 us (30%)
  starting transfers between devices  23.5 us (11%)
  other arithmetic  10.8 us (5%)
  local copies, waits for them, and re-layouts  5.25 us (2%)
    ppermute x8, waiting for transfers between devices, added(): arrived.append(lax.ppermute(total, 'elem', swaps[stage]))  39.1 us
    pallas_call x3, Pallas kernels, spectra_of(): pl.pallas_call(functools.partial(spectral_kernel, scale=scale, classes=cl...  37.3 us
    ppermute x4, waiting for transfers between devices, decoded(): lax.ppermute(part, 'emit', [(z, z ^ gap) for z in range(ne)])  37.1 us
    ppermute x4, waiting for transfers between devices, added(): lax.ppermute(own, 'emit', [(z, z ^ gaps[cls]) for z in range(ne)])  35.3 us
    pallas_call x4, Pallas kernels, steer_blocks(): pl.pallas_call(functools.partial(steer_kernel, cls=cls, tokens=len(after)...  24.3 us
    ppermute x8, starting transfers between devices, added(): arrived.append(lax.ppermute(total, 'elem', swaps[stage]))  11.1 us
    add x12, other arithmetic, added(): total = total + array[start:start + high - low]  9.66 us
    ppermute x4, starting transfers between devices, added(): lax.ppermute(own, 'emit', [(z, z ^ gaps[cls]) for z in range(ne)])  7.56 us
  transfers between devices with their start and end apart: 20, of which 14 were waited for; matrix products, arithmetic and copies ran while one was open for 3% of the time, Pallas kernels for 22%

profile of v2, /device:TPU:0, one launch (start us, length us, event | category | flops | bytes accessed | tf_op | source)
XLA Modules:
  0.0 218.0 jit_solution(7101884221788239023)
XLA Ops:
  3.1 12.5 %spectral.3 = (f32[8,128,8,128]{3,2,1,0:T(8,128)S(1)}, f32[8,128,8,128]{3,2,1,0:T(8,128)S(1)}) custom-call(s32[1]{0:T(128)} %bitcast.2.base_ref, s32[256]{0:T(256)S(1)} %copy-done.10, f32[4,2,128]{2,1,0:T(2,128)S(1)} %copy-done.8, f32[2,528,128]{2,1,0:T(8,128)S(1)} %copy-done.5, f32[64,128,1024]{2,1,0:T(8,128)} %x_hbm.5), custom_call_target="tpu_custom_call" | custom-call | flops 8589934592 | bytes 41943040 | tf_op jit(solution)/shard_map/spectral/pallas_call | solution.py:149
  15.6 5.8 %steer.4 = (f32[4,8,64,256]{3,2,1,0:T(8,128)S(1)}, f32[4,8,64,256]{3,2,1,0:T(8,128)S(1)}) custom-call(s32[8]{0:T(128)S(1)} %fusion.4.target_ref, f32[8,2,64,8,128]{4,3,2,1,0:T(8,128)S(1)} %bitcast.16, f32[64,4,128,256]{3,2,1,0:T(8,128)} %bitcast.26, f32[8,128,8,128]{3,2,1,0:T(8,128)S(1)} %get-tuple-element.35.refs_0_), custom_call_target="tpu_custom_call" | custom-call | flops 1610612736 | bytes 16777216 | tf_op jit(solution)/shard_map/steer/pallas_call | solution.py:214
  22.0 5.8 %steer.5 = (f32[4,8,64,256]{3,2,1,0:T(8,128)S(1)}, f32[4,8,64,256]{3,2,1,0:T(8,128)S(1)}) custom-call(s32[8]{0:T(128)S(1)} %fusion.4.target_ref, f32[8,2,64,8,128]{4,3,2,1,0:T(8,128)S(1)} %bitcast.19, f32[64,4,128,256]{3,2,1,0:T(8,128)} %bitcast.27, f32[4,8,64,256]{3,2,1,0:T(8,128)S(1)} %get-tuple-element.38.refs_0_), custom_call_target="tpu_custom_call" | custom-call | flops 1610612736 | bytes 16777216 | tf_op jit(solution)/shard_map/steer/pallas_call | solution.py:214
  28.0 2.6 %collective-permute-start.1 = (f32[2,8,64,256]{3,2,1,0:T(8,128)S(1)}, f32[2,8,64,256]{3,2,1,0:T(8,128)S(1)}, u32[]{:S(2)}, u32[]{:S(2)}) collective-permute-start(f32[2,8,64,256]{3,2,1,0:T(8,128)S(1)} %slice_add_fusion.3.refs_0_), channel_id=1, source_target_pairs={{0,2},{1,5},{2,0},{3,7},{4,6},{5,1},{6,4},{7,3},{8,10},{9,13},{10,... | collective-permute-start | bytes 3145736 | tf_op jit(solution)/shard_map/ppermute | solution.py:353
  30.8 12.4 %spectral.4 = f32[8,128,8,128]{3,2,1,0:T(8,128)S(1)} custom-call(s32[1]{0:T(128)} %bitcast.2.base_ref, s32[256]{0:T(256)S(1)} %copy-done.11, f32[4,2,128]{2,1,0:T(2,128)S(1)} %copy-done.9, f32[1,528,128]{2,1,0:T(8,128)S(1)} %copy-done.7, f32[64,128,1024]{2,1,0:T(8,128)} %x_hbm.5, f32[2,8,64,256]{3,2,1,0:T(8,128)S(1)} %slice_add_fusion.3.refs_0_), custom_call_target="tpu_custom_call" | custom-call | flops 6442450944 | bytes 37748736 | tf_op jit(solution)/shard_map/spectral/pallas_call | solution.py:149
  43.4 5.8 %steer.6 = (f32[4,8,64,256]{3,2,1,0:T(8,128)S(1)}, f32[4,8,64,256]{3,2,1,0:T(8,128)S(1)}) custom-call(s32[8]{0:T(128)S(1)} %fusion.4.target_ref, f32[8,2,64,8,128]{4,3,2,1,0:T(8,128)S(1)} %bitcast.15, f32[64,4,128,256]{3,2,1,0:T(8,128)} %bitcast.28, f32[1,8,64,256]{3,2,1,0:T(8,128)S(1)} %slice_add_fusion.18.refs_0_), custom_call_target="tpu_custom_call" | custom-call | flops 1610612736 | bytes 16777216 | tf_op jit(solution)/shard_map/steer/pallas_call | solution.py:214
  49.4 2.0 collective-permute-start.2
  51.4 7.2 %collective-permute-done.2 = f32[1,8,64,256]{3,2,1,0:T(8,128)S(1)} collective-permute-done((f32[1,8,64,256]{3,2,1,0:T(8,128)S(1)}, f32[1,8,64,256]{3,2,1,0:T(8,128)S(1)}, u32[]{:S(2)}, u32[]{:S(2)}) %collective-permute-start.2) | collective-permute-done | bytes 524320 | tf_op jit(solution)/shard_map/ppermute | solution.py:353
  58.9 2.0 collective-permute-start.6
  61.0 1.3 copy-done.12
  62.4 12.4 %spectral.5.refs_0_ = f32[8,128,8,128]{3,2,1,0:T(8,128)S(1)} custom-call(s32[1]{0:T(128)} %bitcast.2.base_ref, s32[256]{0:T(256)S(1)} %copy-done.11, f32[4,2,128]{2,1,0:T(2,128)S(1)} %copy-done.9, f32[1,528,128]{2,1,0:T(8,128)S(1)} %copy-done.6, f32[64,128,1024]{2,1,0:T(8,128)} %x_hbm.5, f32[2,8,64,256]{3,2,1,0:T(8,128)S(1)} %slice_add_fusion.1.refs_0_), custom_call_target="tpu_custom_call" | custom-call | flops 6442450944 | bytes 37748736 | tf_op jit(solution)/shard_map/spectral/pallas_call | solution.py:149
  74.8 6.9 %steer.7 = (f32[4,8,64,256]{3,2,1,0:T(8,128)}, f32[4,8,64,256]{3,2,1,0:T(8,128)S(1)}) custom-call(s32[8]{0:T(128)S(1)} %fusion.4.target_ref, f32[8,2,64,8,128]{4,3,2,1,0:T(8,128)S(1)} %bitcast.14, f32[64,4,128,256]{3,2,1,0:T(8,128)} %bitcast.29, f32[8,128,8,128]{3,2,1,0:T(8,128)S(1)} %spectral.5.refs_0_), custom_call_target="tpu_custom_call" | custom-call | flops 1610612736 | bytes 16777216 | tf_op jit(solution)/shard_map/steer/pallas_call | solution.py:214
  81.8 1.4 copy-done.3
  84.2 2.6 %collective-permute-start.3 = (f32[8,64,256]{2,1,0:T(8,128)S(1)}, f32[8,64,256]{2,1,0:T(8,128)S(1)}, u32[]{:S(2)}, u32[]{:S(2)}) collective-permute-start(f32[8,64,256]{2,1,0:T(8,128)S(1)} %bitcast.20), channel_id=1, source_target_pairs={{0,16},{8,24},{16,0},{24,8},{1,17},{9,25},{17,1},{25,9},{2,18},{10... | collective-permute-start | bytes 1572872 | tf_op jit(solution)/shard_map/ppermute | solution.py:357
  86.8 1.5 slice_add_fusion.14
  88.3 1.3 collective-permute-start.9
  89.8 13.8 %collective-permute-done.7 = f32[2,8,64,256]{3,2,1,0:T(8,128)S(1)} collective-permute-done((f32[2,8,64,256]{3,2,1,0:T(8,128)S(1)}, f32[2,8,64,256]{3,2,1,0:T(8,128)S(1)}, u32[]{:S(2)}, u32[]{:S(2)}) %collective-permute-start.7) | collective-permute-done | bytes 1048608 | tf_op jit(solution)/shard_map/ppermute | solution.py:353
  104.7 6.4 %collective-permute-done.3.near_ref = f32[8,64,256]{2,1,0:T(8,128)S(1)} collective-permute-done((f32[8,64,256]{2,1,0:T(8,128)S(1)}, f32[8,64,256]{2,1,0:T(8,128)S(1)}, u32[]{:S(2)}, u32[]{:S(2)}) %collective-permute-start.3) | collective-permute-done | bytes 524320 | tf_op jit(solution)/shard_map/ppermute | solution.py:357
  111.6 1.5 fusion.2
  113.1 1.4 slice_add_fusion
  115.5 14.4 %collective-permute-done.11 = f32[1,8,64,256]{3,2,1,0:T(8,128)S(1)} collective-permute-done((f32[1,8,64,256]{3,2,1,0:T(8,128)S(1)}, f32[1,8,64,256]{3,2,1,0:T(8,128)S(1)}, u32[]{:S(2)}, u32[]{:S(2)}) %collective-permute-start.11) | collective-permute-done | bytes 524320 | tf_op jit(solution)/shard_map/ppermute | solution.py:353
  131.8 2.3 %collective-permute-done.13 = f32[2,8,64,256]{3,2,1,0:T(8,128)S(1)} collective-permute-done((f32[2,8,64,256]{3,2,1,0:T(8,128)S(1)}, f32[2,8,64,256]{3,2,1,0:T(8,128)S(1)}, u32[]{:S(2)}, u32[]{:S(2)}) %collective-permute-start.13) | collective-permute-done | bytes 1048608 | tf_op jit(solution)/shard_map/ppermute | solution.py:353
  135.3 1.4 collective-permute-start.16
  136.8 6.1 %collective-permute-done.12.near_ref = f32[8,64,256]{2,1,0:T(8,128)S(1)} collective-permute-done((f32[8,64,256]{2,1,0:T(8,128)S(1)}, f32[8,64,256]{2,1,0:T(8,128)S(1)}, u32[]{:S(2)}, u32[]{:S(2)}) %collective-permute-start.12) | collective-permute-done | bytes 524320 | tf_op jit(solution)/shard_map/ppermute | solution.py:357
  143.3 1.2 collective-permute-done.16
  144.5 1.2 fusion.refs_0_
  146.6 3.4 %collective-permute-start.15 = (f32[8,64,256]{2,1,0:T(8,128)S(1)}, f32[8,64,256]{2,1,0:T(8,128)S(1)}, u32[]{:S(2)}, u32[]{:S(2)}) collective-permute-start(f32[8,64,256]{2,1,0:T(8,128)S(1)} %bitcast.22), channel_id=1, source_target_pairs={{0,16},{8,24},{16,0},{24,8},{1,17},{9,25},{17,1},{25,9},{2,18},{10... | collective-permute-start | bytes 1572872 | tf_op jit(solution)/shard_map/ppermute | solution.py:357
  150.7 22.1 %collective-permute-done.17.near_ref = f32[8,64,256]{2,1,0:T(8,128)S(1)} collective-permute-done((f32[8,64,256]{2,1,0:T(8,128)S(1)}, f32[8,64,256]{2,1,0:T(8,128)S(1)}, u32[]{:S(2)}, u32[]{:S(2)}) %collective-permute-start.17) | collective-permute-done | bytes 524320 | tf_op jit(solution)/shard_map/ppermute | solution.py:357
  174.6 3.0 %collective-permute-start.19 = (f32[8,64,256]{2,1,0:T(8,128)S(1)}, f32[8,64,256]{2,1,0:T(8,128)S(1)}, u32[]{:S(2)}, u32[]{:S(2)}) collective-permute-start(f32[8,64,256]{2,1,0:T(8,128)S(1)} %get-tuple-element.61.refs_0_), channel_id=1, source_target_pairs={{0,16},{8,24},{16,0},{24,8},{1,17},{9,25},{17,1},{25,9},{2,18},{10... | collective-permute-start | bytes 1572872 | tf_op jit(solution)/shard_map/ppermute | solution.py:366
  177.6 17.7 %collective-permute-done.8.refs_1_ = f32[8,64,256]{2,1,0:T(8,128)S(1)} collective-permute-done((f32[8,64,256]{2,1,0:T(8,128)S(1)}, f32[8,64,256]{2,1,0:T(8,128)S(1)}, u32[]{:S(2)}, u32[]{:S(2)}) %collective-permute-start.8) | collective-permute-done | bytes 524320 | tf_op jit(solution)/shard_map/ppermute | solution.py:366
  197.4 17.3 %collective-permute-done.18.refs_2_ = f32[8,64,256]{2,1,0:T(8,128)S(1)} collective-permute-done((f32[8,64,256]{2,1,0:T(8,128)S(1)}, f32[8,64,256]{2,1,0:T(8,128)S(1)}, u32[]{:S(2)}, u32[]{:S(2)}) %collective-permute-start.18) | collective-permute-done | bytes 524320 | tf_op jit(solution)/shard_map/ppermute | solution.py:366
  215.6 1.6 collective-permute-done.19.refs_2_
  (73 shorter events, 19.7 us)
Async XLA Ops:
  21.4 6.4 %collective-permute-start = (f32[4,8,64,256]{3,2,1,0:T(8,128)S(1)}, f32[4,8,64,256]{3,2,1,0:T(8,128)S(1)}, u32[]{:S(2)}, u32[]{:S(2)}) collective-permute-start(f32[4,8,64,256]{3,2,1,0:T(8,128)S(1)} %get-tuple-element.38.refs_0_), channel_id=1, source_target_pairs={{0,1},{1,0},{2,3},{3,2},{4,5},{5,4},{6,7},{7,6},{8,9},{9,8},{10,11... | collective-permute-start | bytes 6291464 | tf_op jit(solution)/shard_map/ppermute | solution.py:338
  27.7 31.0 %copy-start = (f32[4,8,64,256]{3,2,1,0:T(8,128)}, f32[4,8,64,256]{3,2,1,0:T(8,128)S(1)}, u32[]{:S(2)}) copy-start(f32[4,8,64,256]{3,2,1,0:T(8,128)S(1)} %get-tuple-element.54) | copy-start | bytes 6291460
  27.8 3.0 %copy-start.7 = (f32[1,528,128]{2,1,0:T(8,128)S(1)}, f32[1,528,128]{2,1,0:T(8,128)}, u32[]{:S(2)}) copy-start(f32[1,528,128]{2,1,0:T(8,128)} %constant.34.clone.table_ref) | copy-start | bytes 811012
  27.8 3.0 %copy-start.9 = (f32[4,2,128]{2,1,0:T(2,128)S(1)}, f32[4,2,128]{2,1,0:T(2,128)}, u32[]{:S(2)}) copy-start(f32[4,2,128]{2,1,0:T(2,128)} %codes_ref.5) | copy-start | bytes 12292
  27.8 3.0 %copy-start.11 = (s32[256]{0:T(256)S(1)}, s32[256]{0:T(256)}, u32[]{:S(2)}) copy-start(s32[256]{0:T(256)} %code_ref.5) | copy-start | bytes 3076
  28.0 15.3 %collective-permute-start.1 = (f32[2,8,64,256]{3,2,1,0:T(8,128)S(1)}, f32[2,8,64,256]{3,2,1,0:T(8,128)S(1)}, u32[]{:S(2)}, u32[]{:S(2)}) collective-permute-start(f32[2,8,64,256]{3,2,1,0:T(8,128)S(1)} %slice_add_fusion.3.refs_0_), channel_id=1, source_target_pairs={{0,2},{1,5},{2,0},{3,7},{4,6},{5,1},{6,4},{7,3},{8,10},{9,13},{10,... | collective-permute-start | bytes 3145736 | tf_op jit(solution)/shard_map/ppermute | solution.py:353
  30.5 28.2 %collective-permute-start.4 = (f32[4,8,64,256]{3,2,1,0:T(8,128)S(1)}, f32[4,8,64,256]{3,2,1,0:T(8,128)S(1)}, u32[]{:S(2)}, u32[]{:S(2)}) collective-permute-start(f32[4,8,64,256]{3,2,1,0:T(8,128)S(1)} %get-tuple-element.39), channel_id=1, source_target_pairs={{0,1},{1,0},{2,3},{3,2},{4,5},{5,4},{6,7},{7,6},{8,9},{9,8},{10,11... | collective-permute-start | bytes 6291464 | tf_op jit(solution)/shard_map/ppermute | solution.py:338
  49.2 11.7 %copy-start.1 = (f32[4,8,64,256]{3,2,1,0:T(8,128)}, f32[4,8,64,256]{3,2,1,0:T(8,128)S(1)}, u32[]{:S(2)}) copy-start(f32[4,8,64,256]{3,2,1,0:T(8,128)S(1)} %get-tuple-element.56) | copy-start | bytes 6291460
  49.2 11.7 %collective-permute-start.5 = (f32[4,8,64,256]{3,2,1,0:T(8,128)S(1)}, f32[4,8,64,256]{3,2,1,0:T(8,128)S(1)}, u32[]{:S(2)}, u32[]{:S(2)}) collective-permute-start(f32[4,8,64,256]{3,2,1,0:T(8,128)S(1)} %get-tuple-element.42), channel_id=1, source_target_pairs={{0,1},{1,0},{2,3},{3,2},{4,5},{5,4},{6,7},{7,6},{8,9},{9,8},{10,11... | collective-permute-start | bytes 6291464 | tf_op jit(solution)/shard_map/ppermute | solution.py:338
  49.4 9.2 %collective-permute-start.2 = (f32[1,8,64,256]{3,2,1,0:T(8,128)S(1)}, f32[1,8,64,256]{3,2,1,0:T(8,128)S(1)}, u32[]{:S(2)}, u32[]{:S(2)}) collective-permute-start(f32[1,8,64,256]{3,2,1,0:T(8,128)S(1)} %slice_add_fusion.18.refs_0_), channel_id=1, source_target_pairs={{0,4},{1,3},{2,6},{3,1},{4,0},{5,7},{6,2},{7,5},{8,12},{9,11},{10,... | collective-permute-start | bytes 1572872 | tf_op jit(solution)/shard_map/ppermute | solution.py:353
  58.8 3.7 %copy-start.13 = (f32[4,8,64,256]{3,2,1,0:T(8,128)}, f32[4,8,64,256]{3,2,1,0:T(8,128)S(1)}, u32[]{:S(2)}) copy-start(f32[4,8,64,256]{3,2,1,0:T(8,128)S(1)} %collective-permute-done.4) | copy-start | bytes 6291460
  58.9 3.5 %copy-start.6 = (f32[1,528,128]{2,1,0:T(8,128)S(1)}, f32[1,528,128]{2,1,0:T(8,128)}, u32[]{:S(2)}) copy-start(f32[1,528,128]{2,1,0:T(8,128)} %constant.35.clone.table_ref) | copy-start | bytes 811012
  58.9 27.9 %collective-permute-start.6 = (f32[2,8,64,256]{3,2,1,0:T(8,128)S(1)}, f32[2,8,64,256]{3,2,1,0:T(8,128)}, u32[]{:S(2)}, u32[]{:S(2)}) collective-permute-start(f32[2,8,64,256]{3,2,1,0:T(8,128)S(1)} %slice_add_fusion.2), channel_id=1, source_target_pairs={{0,2},{1,5},{2,0},{3,7},{4,6},{5,1},{6,4},{7,3},{8,10},{9,13},{10,... | collective-permute-start | bytes 3145736 | tf_op jit(solution)/shard_map/ppermute | solution.py:353
  61.0 1.3 copy-start.12
  74.8 9.2 %copy-start.14 = (s32[256]{0:T(256)S(1)}, s32[256]{0:T(256)}, u32[]{:S(2)}) copy-start(s32[256]{0:T(256)} %param.13) | copy-start | bytes 3076
  81.8 1.4 copy-start.3
  83.2 29.9 %collective-permute-start.10 = (f32[4,8,64,256]{3,2,1,0:T(8,128)}, f32[4,8,64,256]{3,2,1,0:T(8,128)}, u32[]{:S(2)}, u32[]{:S(2)}) collective-permute-start(f32[4,8,64,256]{3,2,1,0:T(8,128)} %get-tuple-element.48), channel_id=1, source_target_pairs={{0,1},{1,0},{2,3},{3,2},{4,5},{5,4},{6,7},{7,6},{8,9},{9,8},{10,11... | collective-permute-start | bytes 6291464 | tf_op jit(solution)/shard_map/ppermute | solution.py:338
  83.2 20.4 %copy-start.2 = (f32[4,8,64,256]{3,2,1,0:T(8,128)S(1)}, f32[4,8,64,256]{3,2,1,0:T(8,128)}, u32[]{:S(2)}) copy-start(f32[4,8,64,256]{3,2,1,0:T(8,128)} %copy-done.1) | copy-start | bytes 6291460
  83.2 20.4 %collective-permute-start.7 = (f32[2,8,64,256]{3,2,1,0:T(8,128)S(1)}, f32[2,8,64,256]{3,2,1,0:T(8,128)S(1)}, u32[]{:S(2)}, u32[]{:S(2)}) collective-permute-start(f32[2,8,64,256]{3,2,1,0:T(8,128)S(1)} %slice_add_fusion.1.refs_0_), channel_id=1, source_target_pairs={{0,2},{1,5},{2,0},{3,7},{4,6},{5,1},{6,4},{7,3},{8,10},{9,13},{10,... | collective-permute-start | bytes 3145736 | tf_op jit(solution)/shard_map/ppermute | solution.py:353
  84.2 26.9 %collective-permute-start.3 = (f32[8,64,256]{2,1,0:T(8,128)S(1)}, f32[8,64,256]{2,1,0:T(8,128)S(1)}, u32[]{:S(2)}, u32[]{:S(2)}) collective-permute-start(f32[8,64,256]{2,1,0:T(8,128)S(1)} %bitcast.20), channel_id=1, source_target_pairs={{0,16},{8,24},{16,0},{24,8},{1,17},{9,25},{17,1},{25,9},{2,18},{10... | collective-permute-start | bytes 1572872 | tf_op jit(solution)/shard_map/ppermute | solution.py:357
  88.3 23.3 %collective-permute-start.9 = (f32[1,8,64,256]{3,2,1,0:T(8,128)S(1)}, f32[1,8,64,256]{3,2,1,0:T(8,128)S(1)}, u32[]{:S(2)}, u32[]{:S(2)}) collective-permute-start(f32[1,8,64,256]{3,2,1,0:T(8,128)S(1)} %slice_add_fusion.14), channel_id=1, source_target_pairs={{0,4},{1,3},{2,6},{3,1},{4,0},{5,7},{6,2},{7,5},{8,12},{9,11},{10,... | collective-permute-start | bytes 1572872 | tf_op jit(solution)/shard_map/ppermute | solution.py:353
  104.7 8.3 %copy-start.4 = (f32[4,8,64,256]{3,2,1,0:T(8,128)S(1)}, f32[4,8,64,256]{3,2,1,0:T(8,128)}, u32[]{:S(2)}) copy-start(f32[4,8,64,256]{3,2,1,0:T(8,128)} %copy-done.3) | copy-start | bytes 6291460
  114.5 19.7 %collective-permute-start.13 = (f32[2,8,64,256]{3,2,1,0:T(8,128)S(1)}, f32[2,8,64,256]{3,2,1,0:T(8,128)S(1)}, u32[]{:S(2)}, u32[]{:S(2)}) collective-permute-start(f32[2,8,64,256]{3,2,1,0:T(8,128)S(1)} %slice_add_fusion), channel_id=1, source_target_pairs={{0,2},{1,5},{2,0},{3,7},{4,6},{5,1},{6,4},{7,3},{8,10},{9,13},{10,... | collective-permute-start | bytes 3145736 | tf_op jit(solution)/shard_map/ppermute | solution.py:353
  115.1 14.8 %collective-permute-start.11 = (f32[1,8,64,256]{3,2,1,0:T(8,128)S(1)}, f32[1,8,64,256]{3,2,1,0:T(8,128)S(1)}, u32[]{:S(2)}, u32[]{:S(2)}) collective-permute-start(f32[1,8,64,256]{3,2,1,0:T(8,128)S(1)} %slice_add_fusion.12.refs_0_), channel_id=1, source_target_pairs={{0,4},{1,3},{2,6},{3,1},{4,0},{5,7},{6,2},{7,5},{8,12},{9,11},{10,... | collective-permute-start | bytes 1572872 | tf_op jit(solution)/shard_map/ppermute | solution.py:353
  131.1 11.8 %collective-permute-start.12 = (f32[8,64,256]{2,1,0:T(8,128)S(1)}, f32[8,64,256]{2,1,0:T(8,128)S(1)}, u32[]{:S(2)}, u32[]{:S(2)}) collective-permute-start(f32[8,64,256]{2,1,0:T(8,128)S(1)} %bitcast.24), channel_id=1, source_target_pairs={{0,8},{8,0},{16,24},{24,16},{1,9},{9,1},{17,25},{25,17},{2,10},{10... | collective-permute-start | bytes 1572872 | tf_op jit(solution)/shard_map/ppermute | solution.py:357
  135.3 9.2 %collective-permute-start.16 = (f32[1,8,64,256]{3,2,1,0:T(8,128)S(1)}, f32[1,8,64,256]{3,2,1,0:T(8,128)S(1)}, u32[]{:S(2)}, u32[]{:S(2)}) collective-permute-start(f32[1,8,64,256]{3,2,1,0:T(8,128)S(1)} %slice_add_fusion.6.refs_0_), channel_id=1, source_target_pairs={{0,4},{1,3},{2,6},{3,1},{4,0},{5,7},{6,2},{7,5},{8,12},{9,11},{10,... | collective-permute-start | bytes 1572872 | tf_op jit(solution)/shard_map/ppermute | solution.py:353
  145.7 27.1 %collective-permute-start.17 = (f32[8,64,256]{2,1,0:T(8,128)S(1)}, f32[8,64,256]{2,1,0:T(8,128)S(1)}, u32[]{:S(2)}, u32[]{:S(2)}) collective-permute-start(f32[8,64,256]{2,1,0:T(8,128)S(1)} %bitcast.17), channel_id=1, source_target_pairs={{0,8},{8,0},{16,24},{24,16},{1,9},{9,1},{17,25},{25,17},{2,10},{10... | collective-permute-start | bytes 1572872 | tf_op jit(solution)/shard_map/ppermute | solution.py:357
  146.6 27.5 %collective-permute-start.15 = (f32[8,64,256]{2,1,0:T(8,128)S(1)}, f32[8,64,256]{2,1,0:T(8,128)S(1)}, u32[]{:S(2)}, u32[]{:S(2)}) collective-permute-start(f32[8,64,256]{2,1,0:T(8,128)S(1)} %bitcast.22), channel_id=1, source_target_pairs={{0,16},{8,24},{16,0},{24,8},{1,17},{9,25},{17,1},{25,9},{2,18},{10... | collective-permute-start | bytes 1572872 | tf_op jit(solution)/shard_map/ppermute | solution.py:357
  149.9 45.3 %collective-permute-start.8 = (f32[8,64,256]{2,1,0:T(8,128)S(1)}, f32[8,64,256]{2,1,0:T(8,128)S(1)}, u32[]{:S(2)}, u32[]{:S(2)}) collective-permute-start(f32[8,64,256]{2,1,0:T(8,128)S(1)} %get-tuple-element.52), channel_id=1, source_target_pairs={{0,8},{8,0},{16,24},{24,16},{1,9},{9,1},{17,25},{25,17},{2,10},{10... | collective-permute-start | bytes 1572872 | tf_op jit(solution)/shard_map/ppermute | solution.py:366
  150.0 46.5 %collective-permute-start.14 = (f32[8,64,256]{2,1,0:T(8,128)S(1)}, f32[8,64,256]{2,1,0:T(8,128)S(1)}, u32[]{:S(2)}, u32[]{:S(2)}) collective-permute-start(f32[8,64,256]{2,1,0:T(8,128)S(1)} %get-tuple-element.59), channel_id=1, source_target_pairs={{0,16},{8,24},{16,0},{24,8},{1,17},{9,25},{17,1},{25,9},{2,18},{10... | collective-permute-start | bytes 1572872 | tf_op jit(solution)/shard_map/ppermute | solution.py:366
  174.5 40.3 %collective-permute-start.18 = (f32[8,64,256]{2,1,0:T(8,128)S(1)}, f32[8,64,256]{2,1,0:T(8,128)S(1)}, u32[]{:S(2)}, u32[]{:S(2)}) collective-permute-start(f32[8,64,256]{2,1,0:T(8,128)S(1)} %get-tuple-element.63), channel_id=1, source_target_pairs={{0,8},{8,0},{16,24},{24,16},{1,9},{9,1},{17,25},{25,17},{2,10},{10... | collective-permute-start | bytes 1572872 | tf_op jit(solution)/shard_map/ppermute | solution.py:366
  174.6 42.6 %collective-permute-start.19 = (f32[8,64,256]{2,1,0:T(8,128)S(1)}, f32[8,64,256]{2,1,0:T(8,128)S(1)}, u32[]{:S(2)}, u32[]{:S(2)}) collective-permute-start(f32[8,64,256]{2,1,0:T(8,128)S(1)} %get-tuple-element.61.refs_0_), channel_id=1, source_target_pairs={{0,16},{8,24},{16,0},{24,8},{1,17},{9,25},{17,1},{25,9},{2,18},{10... | collective-permute-start | bytes 1572872 | tf_op jit(solution)/shard_map/ppermute | solution.py:366
  (3 other events, 2.4 us)
